TPU v7x, 512 devices: a whole 4x4x16 slice. The times are simulated.
512 devices in a mesh: dp: 8 (over y, core), expert: 64 (over x, z).
Axes of the slice: x: 4, y: 4, z: 16, core: 2. Of those that a mesh axis runs over, the one named last changes fastest.
Arguments:
- tokens: bfloat16 [16384, 1024], P('expert', 'dp'), may hold values from -6 to 6
- cotangent: bfloat16 [16384, 1024], P('expert', 'dp'), may hold values from -6 to 6
- expert_ids: int32 [16384, 2], P('expert'), may hold values from 0 to 63, all different within a row; in each aligned block of 256 rows (0 to 255, 256 to 511, ...) at most 12 rows name the same one
- gate_weights: float32 [16384, 2], P('expert'), may hold values from 0.2 to 1
- weight_in: bfloat16 [64, 1024, 4096], P('expert', None, 'dp'), may hold values from -0.1875 to 0.1875
- weight_out: bfloat16 [64, 4096, 1024], P('expert', 'dp'), may hold values from -0.09375 to 0.09375
Outputs:
- output: bfloat16 [16384, 1024], P('expert', 'dp')
- grad_tokens: bfloat16 [16384, 1024], P('expert', 'dp')
- grad_weight_in: bfloat16 [64, 1024, 4096], P('expert', None, 'dp')
- grad_weight_out: bfloat16 [64, 4096, 1024], P('expert', 'dp')
Inputs may be any that keep to these rules, and one draw needn't show every extreme that they name: `expert_ids`: the two experts of a token differ. In each aligned block of 256 rows (the rows of one device along expert) no expert is named by more than 12 rows, a bound that some block reaches.
All inputs are finite; a program needn't handle non-finite values.
Results may differ from a plain program's by a relative error of at most 0.015.
Values may be sent and summed in bfloat16 or wider, within the bound.
No kernel may reach another device: no remote copies, remote signals or barrier semaphores. Data moves between devices by JAX's collectives and lax.ppermute only.
A program may use at most 64 MiB of HBM per device.

v0:
```python
import jax
import jax.numpy as jnp
from jax import lax
from jax.sharding import PartitionSpec as P

half_root = 0.7071067811865476
inv_root_tau = 0.3989422804014327


def sent_together(arrays, axis, split_dim, concat_dim, along):
    ends, at = ([], 0)
    for a in arrays[:-1]:
        at += a.shape[along]
        ends.append(at)
    both = jnp.concatenate(arrays, axis=along)
    return tuple(
        jnp.split(
            lax.all_to_all(both, axis, split_axis=split_dim, concat_axis=concat_dim, tiled=True),
            ends,
            axis=along,
        )
    )


def side_by_side(arrays, axis, dim, along):
    ends, at = ([], 0)
    for a in arrays[:-1]:
        at += a.shape[along]
        ends.append(at)
    both = jnp.concatenate(arrays, axis=along)
    return tuple(jnp.split(lax.all_gather(both, axis, axis=dim, tiled=True), ends, axis=along))


def in_blocks(x, dim, peers):
    before, after = (x.shape[:dim], x.shape[dim + 1 :])
    return jnp.moveaxis(x.reshape(*before, peers, -1, *after), dim, 0)


def summed_on_arrival(x, axis, dim):
    peers = lax.axis_size(axis)
    tiles = lax.all_to_all(in_blocks(x, dim, peers), axis, 0, 0, tiled=True)
    return jnp.sum(tiles.astype(jnp.float32), axis=0)


def in_one_piece(arrays, axis, dim, along):
    both = jnp.concatenate(arrays, axis=along)
    filled, at, done = (summed_on_arrival(both, axis, dim), 0, [])
    for a in arrays:
        done.append(lax.slice_in_dim(filled, at, at + a.shape[along], axis=along))
        at += a.shape[along]
    return tuple(done)


def gelu_exact(value):
    return 0.5 * value * (1.0 + jax.scipy.special.erf(value * half_root))


def gelu_slope(value):
    return 0.5 * (1.0 + jax.scipy.special.erf(value * half_root)) + value * inv_root_tau * jnp.exp(
        -0.5 * value * value
    )


def contract(left, right, left_dim, right_dim):
    return lax.dot_general(
        left, right, (((left_dim,), (right_dim,)), ((), ())), preferred_element_type=jnp.float32
    )


def slot_owner(block_ids, capacity, experts):
    flat_ids = block_ids.reshape(-1)
    count = flat_ids.shape[0]
    onehot = (flat_ids[:, None] == jnp.arange(experts, dtype=jnp.int32)[None, :]).astype(jnp.int32)
    position = jnp.sum(jnp.cumsum(onehot, axis=0) * onehot, axis=1) - 1
    slot_index = flat_ids * capacity + position
    owner_of = (
        jnp.full((experts * capacity,), -1, jnp.int32)
        .at[slot_index]
        .set(jnp.arange(count, dtype=jnp.int32))
    )
    return (slot_index, owner_of)


def expert_work(inputs, scaled, w_in_slice, w_out_slice):
    pre_act = jnp.dot(inputs, w_in_slice, preferred_element_type=jnp.float32)
    hidden = gelu_exact(pre_act).astype(jnp.bfloat16)
    out_part = jnp.dot(hidden, w_out_slice, preferred_element_type=jnp.float32).astype(jnp.bfloat16)
    grad_hidden = contract(scaled, w_out_slice, 1, 1)
    d_pre = (grad_hidden * gelu_slope(pre_act)).astype(jnp.bfloat16)
    back_part = contract(d_pre, w_in_slice, 1, 1).astype(jnp.bfloat16)
    grad_out = contract(hidden, scaled, 0, 0).astype(jnp.bfloat16)
    grad_in = contract(inputs, d_pre, 0, 0).astype(jnp.bfloat16)
    return (out_part, back_part, grad_in, grad_out)


def on_device(tokens, cotangent, expert_ids, gate_weights, weight_in, weight_out):
    experts = lax.axis_size("expert")
    tok_rows = tokens.shape[0]
    capacity = 3 * tok_rows // experts
    slot_index, owner_of = slot_owner(expert_ids, capacity, experts)
    filled = (owner_of >= 0)[:, None]
    safe_owner = jnp.maximum(owner_of, 0)
    token_rows = safe_owner // 2
    gate_flat = gate_weights.reshape(-1)
    nothing = jnp.zeros((), jnp.bfloat16)
    w_in_slice = weight_in[0]
    w_out_slice = weight_out[0]
    narrow = tokens.shape[1]
    scaled = (
        (gate_weights[:, :, None] * cotangent[:, None, :].astype(jnp.float32))
        .astype(jnp.bfloat16)
        .reshape(2 * tok_rows, narrow)
    )
    send_inputs = jnp.where(filled, tokens[token_rows], nothing).reshape(experts, capacity, narrow)
    send_scaled = jnp.where(filled, scaled[safe_owner], nothing).reshape(experts, capacity, narrow)
    got_inputs, got_scaled = sent_together((send_inputs, send_scaled), "expert", 0, 0, 1)
    full_inputs, full_scaled = side_by_side(
        (got_inputs.reshape(-1, narrow), got_scaled.reshape(-1, narrow)), "dp", 1, 0
    )
    out_part, back_part, grad_in, grad_out = expert_work(
        full_inputs, full_scaled, w_in_slice, w_out_slice
    )
    out_rows, back_rows = in_one_piece(
        (
            out_part.astype(jnp.float32).astype(jnp.bfloat16),
            back_part.astype(jnp.float32).astype(jnp.bfloat16),
        ),
        "dp",
        1,
        0,
    )
    ret_out, ret_back = tuple(
        (
            part.astype(jnp.float32)
            for part in sent_together(
                (
                    out_rows.reshape(experts, capacity, narrow).astype(jnp.bfloat16),
                    back_rows.reshape(experts, capacity, narrow).astype(jnp.bfloat16),
                ),
                "expert",
                0,
                0,
                1,
            )
        )
    )
    mine_out = ret_out.reshape(-1, narrow)[slot_index]
    mine_back = ret_back.reshape(-1, narrow)[slot_index]
    output = jnp.sum((gate_flat[:, None] * mine_out).reshape(tok_rows, 2, narrow), axis=1)
    grad_tokens = jnp.sum(mine_back.reshape(tok_rows, 2, narrow), axis=1)
    return (
        output.astype(jnp.bfloat16),
        grad_tokens.astype(jnp.bfloat16),
        grad_in[None],
        grad_out[None],
    )


def solution(mesh):
    return jax.shard_map(
        on_device,
        mesh=mesh,
        in_specs=(
            P("expert", "dp"),
            P("expert", "dp"),
            P("expert", None),
            P("expert", None),
            P("expert", None, "dp"),
            P("expert", "dp", None),
        ),
        out_specs=(
            P("expert", "dp"),
            P("expert", "dp"),
            P("expert", None, "dp"),
            P("expert", "dp", None),
        ),
        check_vma=False,
    )
```

profile of v0, /device:TPU:6, one launch (start us, length us, event | category | flops | bytes accessed | tf_op | source)
XLA Modules:
  0.0 203.2 jit_solution(1297681555488745721)
XLA Ops:
  7.2 0.0 copy-start
  7.2 0.0 copy-start.1
  7.2 0.0 all-gather.2.cloned.1.call-start
  7.2 0.8 broadcast_multiply_fusion
  8.0 0.8 copy.19
  8.8 0.1 eq.29
  9.0 0.1 eq.25
  9.1 0.1 copy.18
  9.3 0.1 mul.83
  9.4 0.0 copy-start.2
  9.4 1.2 reduce-window.6
  10.6 0.2 slice_reduce_fusion
  10.9 0.1 fusion.21
  11.1 2.4 %scatter_custom_fusion = s32[768]{0:T(1024)S(1)} fusion(s32[512]{0:T(512)S(1)} %bitcast.51, s32[512]{0:T(512)S(1)} %iota.11, s32[]{:T(128)} %constant.15.clone.1), kind=kCustom, calls=%fused_computation.58 | custom fusion | bytes 3076 | tf_op jit(solution)/shard_map/scatter | solution.py:79
  13.6 0.8 copy.17
  14.4 0.1 mul.85
  14.5 0.1 broadcast_in_dim.41
  14.7 0.0 copy-done.1
  14.7 1.9 gather_fusion
  16.6 0.0 copy-done.2
  16.6 0.1 mul.87
  16.7 0.1 multiply_convert_fusion.1
  16.8 1.9 gather_fusion.1
  18.8 0.2 broadcast_select_fusion.1
  19.0 0.1 pad_maximum_fusion
  19.1 44.9 %all_to_all.15 = bf16[64,24,128]{2,1,0:T(8,128)(2,1)S(1)} all-to-all(bf16[64,24,128]{2,1,0:T(8,128)(2,1)S(1)} %pad_maximum_fusion), channel_id=1, replica_groups=mesh['dp'=8,'expert'=64] {'expert'}, dimensions={0} | all-to-all | bytes 786432 | tf_op jit(solution)/shard_map/all_to_all | solution.py:18
  64.0 0.1 fusion.27
  64.2 0.8 pad_maximum_fusion.1
  65.0 0.0 all-gather.2.cloned.1.call-update
  65.0 0.0 copy-start.5
  65.0 31.2 %all-gather.2.cloned.1.call-done = bf16[1536,1024]{1,0:T(8,128)(2,1)} async-done(((bf16[1536,128]{1,0:T(8,128)(2,1)}), bf16[1536,1024]{1,0:T(8,128)(2,1)}) %all-gather.2.cloned.1.call-update) | async-done | bytes 3145744 | tf_op jit(solution)/shard_map/all_gather | solution.py:31
  96.2 0.0 copy-done
  96.2 2.5 %multiply_convert_fusion = (bf16[768,512]{1,0:T(8,128)(2,1)S(1)}, f32[768,512]{1,0:T(8,128)S(1)}) fusion(bf16[1,1024,512]{2,1,0:T(8,128)(2,1)S(1)} %copy-done, bf16[1536,1024]{1,0:T(8,128)(2,1)} %all-gather.2.cloned.1.call-done), kind=kOutput, calls=%fused_computation.15 | convolution fusion | flops 807272448 | bytes 4980736 | tf_op jit(solution)/shard_map/dot_general | solution.py:85
  98.7 0.0 copy-done.5
  98.7 0.0 copy-start.3
  98.7 1.0 convolution_convert_fusion.1
  99.7 0.9 copy-done.3
  100.6 1.4 fusion.4
  102.0 0.0 copy-start.6
  102.0 0.9 copy-done.6
  102.9 1.0 convolution_convert_fusion
  103.9 0.6 bitcast_bitcast_fusion
  104.5 42.3 %all_to_all.16 = bf16[8,1536,128]{2,1,0:T(8,128)(2,1)} all-to-all(bf16[8,1536,128]{2,1,0:T(8,128)(2,1)S(1)} %bitcast_bitcast_fusion), channel_id=1, replica_groups=mesh['dp'=8,'expert'=64] {'dp'}, dimensions={0} | all-to-all | bytes 6291456 | tf_op jit(solution)/shard_map/all_to_all | solution.py:41
  146.8 2.5 %reduce = bf16[1536,128]{1,0:T(8,128)(2,1)S(1)} reduce(bf16[8,1536,128]{2,1,0:T(8,128)(2,1)} %all_to_all.16, bf16[]{:T(256)} %constant.41.clone.1), dimensions={0}, to_apply=%region_4.5.clone | reduce | flops 1376256 | bytes 3538946 | tf_op jit(solution)/shard_map/reduce_sum | solution.py:42
  149.5 0.9 pad_maximum_fusion.2
  150.3 15.9 %all-to-all-start.2 = ((bf16[64,24,128]{2,1,0:T(8,128)(2,1)}), bf16[64,24,128]{2,1,0:T(8,128)(2,1)S(1)}, u32[]{:S(2)}, u32[]{:S(2)}) async-start(bf16[64,24,128]{2,1,0:T(8,128)(2,1)} %pad_maximum_fusion.2), calls=%async_computation.2 | async-start | bytes 786432 | tf_op jit(solution)/shard_map/all_to_all | solution.py:18
  166.3 0.0 copy-start.4
  166.3 0.0 copy-start.7
  166.3 3.6 %fusion.13 = bf16[1,512,1024]{2,1,0:T(8,128)(2,1)} fusion(bf16[768,512]{1,0:T(8,128)(2,1)S(1)} %get-tuple-element.14, bf16[1536,1024]{1,0:T(8,128)(2,1)} %all-gather.2.cloned.1.call-done), kind=kOutput, calls=%fused_computation.25 | convolution fusion | flops 805830656 | bytes 3407872 | tf_op jit(solution)/shard_map/dot_general | solution.py:65
  169.8 0.0 copy-done.4
  169.8 0.0 copy-done.7
  169.8 2.0 fusion.10
  171.8 20.3 %all-to-all-done.2 = bf16[64,24,128]{2,1,0:T(8,128)(2,1)S(1)} async-done(((bf16[64,24,128]{2,1,0:T(8,128)(2,1)}), bf16[64,24,128]{2,1,0:T(8,128)(2,1)S(1)}, u32[]{:S(2)}, u32[]{:S(2)}) %all-to-all-start.2) | async-done | bytes 393248 | tf_op jit(solution)/shard_map/all_to_all | solution.py:18
  192.1 0.1 slice_convert_fusion
  192.3 1.0 gather_fusion.3
  193.3 1.0 gather_fusion.2
  194.3 1.0 multiply_reduce_fusion
  195.4 0.9 reduce_sum.39
  (19 shorter events, 0.5 us)
Async XLA Ops:
  7.2 89.1 %copy-start = (bf16[1,1024,512]{2,1,0:T(8,128)(2,1)S(1)}, bf16[1,1024,512]{2,1,0:T(8,128)(2,1)}, u32[]{:S(2)}) copy-start(bf16[1,1024,512]{2,1,0:T(8,128)(2,1)} %param.10) | copy-start | bytes 3145732
  7.2 7.5 %copy-start.1 = (bf16[256,128]{1,0:T(8,128)(2,1)S(1)}, bf16[256,128]{1,0:T(8,128)(2,1)}, u32[]{:S(2)}) copy-start(bf16[256,128]{1,0:T(8,128)(2,1)} %param.6) | copy-start | bytes 196612
  7.2 89.0 %all-gather.2.cloned.1.call-start = ((), (), s32[]{:S(2)}) async-start(), calls=%async_computation.3 | async-start | bytes 3538944 | tf_op jit(solution)/shard_map/all_gather | solution.py:31
  9.4 7.2 %copy-start.2 = (bf16[256,128]{1,0:T(8,128)(2,1)S(1)}, bf16[256,128]{1,0:T(8,128)(2,1)}, u32[]{:S(2)}) copy-start(bf16[256,128]{1,0:T(8,128)(2,1)} %param.7) | copy-start | bytes 196612
  65.0 33.7 %copy-start.5 = (bf16[1,512,1024]{2,1,0:T(8,128)(2,1)S(1)}, bf16[1,512,1024]{2,1,0:T(8,128)(2,1)}, u32[]{:S(2)}) copy-start(bf16[1,512,1024]{2,1,0:T(8,128)(2,1)} %param.11) | copy-start | bytes 3145732
  98.7 1.9 copy-start.3
  102.0 0.9 copy-start.6
  150.3 41.8 %all-to-all-start.2 = ((bf16[64,24,128]{2,1,0:T(8,128)(2,1)}), bf16[64,24,128]{2,1,0:T(8,128)(2,1)S(1)}, u32[]{:S(2)}, u32[]{:S(2)}) async-start(bf16[64,24,128]{2,1,0:T(8,128)(2,1)} %pad_maximum_fusion.2), calls=%async_computation.2 | async-start | bytes 786432 | tf_op jit(solution)/shard_map/all_to_all | solution.py:18
  166.3 3.6 %copy-start.4 = (bf16[1536,1024]{1,0:T(8,128)(2,1)S(1)}, bf16[1536,1024]{1,0:T(8,128)(2,1)}, u32[]{:S(2)}) copy-start(bf16[1536,1024]{1,0:T(8,128)(2,1)} %all-gather.2.cloned.1.call-done) | copy-start | bytes 9437188
  166.3 3.6 %copy-start.7 = (bf16[768,512]{1,0:T(8,128)(2,1)S(1)}, bf16[768,512]{1,0:T(8,128)(2,1)}, u32[]{:S(2)}) copy-start(bf16[768,512]{1,0:T(8,128)(2,1)} %copy-done.6) | copy-start | bytes 2359300
Sparse Core Ops, SparseCore 0:
  65.1 31.0 all-gather.1
where the time goes:
time: 204 us; the launch traced here: 203 us
  blocking collectives  87.2 us (43%)
  waiting for transfers between devices  51.5 us (25%)
  starting transfers between devices  15.9 us (8%)
  between operations  14.4 us (7%)
  local copies, waits for them, and re-layouts  13.3 us (7%)
  matrix products  11.4 us (6%)
  other arithmetic  9.45 us (5%)
    all_to_all x1, blocking collectives, sent_together(): lax.all_to_all(both, axis, split_axis=split_dim, concat_axis=concat_dim,...  44.9 us
    all_to_all x1, blocking collectives, summed_on_arrival(): tiles = lax.all_to_all(in_blocks(x, dim, peers), axis, 0, 0, tiled=True)  42.3 us
    all_gather x1, waiting for transfers between devices, side_by_side(): lax.all_gather(both, axis, axis=dim, tiled=True)  31.2 us
    all_to_all x1, waiting for transfers between devices, sent_together(): lax.all_to_all(both, axis, split_axis=split_dim, concat_axis=concat_dim,...  20.3 us
    all_to_all x1, starting transfers between devices, sent_together(): lax.all_to_all(both, axis, split_axis=split_dim, concat_axis=concat_dim,...  15.9 us
    dot_general x4, matrix products, contract(): lax.dot_general(left, right, (((left_dim,), (right_dim,)), ((), ())), pre...  7.93 us
  transfers between devices with their start and end apart: 2, of which 2 were waited for; matrix products, arithmetic and copies ran while one was open for 3% of the time, Pallas kernels for 0%

commit v1 on v0

v1 whole, which is shorter than its diff:
```python
import jax
import jax.numpy as jnp
from jax import lax
from jax.experimental import pallas as pl
from jax.experimental.pallas import tpu as pltpu
from jax.sharding import Mesh, PartitionSpec as P

half_root = 0.7071067811865476
inv_root_tau = 0.3989422804014327

XZ = ("x", "z")
bf16 = jnp.bfloat16
f32 = jnp.float32


def dot(left, right, left_dim=1, right_dim=0):
    return lax.dot_general(
        left, right, (((left_dim,), (right_dim,)), ((), ())), preferred_element_type=f32
    )


def iota(shape, dim):
    return lax.broadcasted_iota(jnp.int32, shape, dim)


def gate_columns(gates_ref):
    rows = jnp.concatenate([gates_ref[...], jnp.zeros((6, gates_ref.shape[1]), f32)], axis=0)
    return jnp.transpose(rows)


def dispatch_kernel(ids_ref, gates_ref, tok_ref, cot_ref, send_ref, pick_ref):
    experts, _, group, _ = send_ref.shape
    rows = tok_ref.shape[0]
    ids = ids_ref[...]
    which = iota((experts, rows), 0)
    first = which == ids[0:1, :]
    second = which == ids[1:2, :]
    member = jnp.where(first | second, 1.0, 0.0).astype(bf16)
    earlier = jnp.where(iota((rows, rows), 0) < iota((rows, rows), 1), 1.0, 0.0).astype(bf16)
    rank = dot(member, earlier)
    ranks = jnp.concatenate(
        [jnp.where(first, rank, -1.0), jnp.where(second, rank, -1.0)], axis=1
    ).astype(bf16)
    slots = experts * group
    at = iota((slots, experts), 0) - group * iota((slots, experts), 1)
    owner = jnp.where((at >= 0) & (at < group), 1.0, 0.0).astype(bf16)
    spread = dot(owner, ranks)
    lane = iota((slots, 2 * rows), 0) & (group - 1)
    low = jnp.where(spread == lane.astype(f32), 1.0, 0.0).astype(bf16)
    high = jnp.where(spread == (8 + (lane & 3)).astype(f32), 1.0, 0.0).astype(bf16)
    pick_ref[0:slots, :] = low
    pick_ref[slots : 2 * slots, :] = high
    gates = gate_columns(gates_ref)
    cot = cot_ref[...].astype(f32)
    tok = tok_ref[...]
    source = jnp.concatenate(
        [
            jnp.concatenate([tok, (gates[:, 0:1] * cot).astype(bf16)], axis=1),
            jnp.concatenate([tok, (gates[:, 1:2] * cot).astype(bf16)], axis=1),
        ],
        axis=0,
    )
    width = tok.shape[1]
    chosen = dot(low, source).astype(bf16)
    rest = dot(high, source)
    mixed = jnp.where((iota((slots, width), 0) & 7) < 4, rest[:, :width], rest[:, width:])
    send_ref[:, 0] = chosen[:, :width].reshape(experts, group, width)
    send_ref[:, 1] = chosen[:, width:].reshape(experts, group, width)
    send_ref[:, 2] = mixed.astype(bf16).reshape(experts, group, width)


def dispatch(ids, gates, tokens, cotangent, experts):
    rows, width = tokens.shape
    return pl.pallas_call(
        dispatch_kernel,
        out_shape=(
            jax.ShapeDtypeStruct((experts, 3, 8, width), bf16),
            jax.ShapeDtypeStruct((experts * 16, 2 * rows), bf16),
        ),
        name="dispatch",
    )(ids.T, gates.T, tokens, cotangent)


def combine_kernel(pick_ref, gates_ref, ret_ref, out_ref, grad_ref):
    experts, _, group, width = ret_ref.shape
    rows = out_ref.shape[0]
    slots = experts * group
    tail = ret_ref[:, 2].reshape(slots, width)
    is_out = (iota((slots, width), 0) & 7) < 4
    nothing = jnp.zeros((slots, width), f32)
    tail = tail.astype(f32)
    low = jnp.concatenate(
        [ret_ref[:, 0].reshape(slots, width), ret_ref[:, 1].reshape(slots, width)], axis=1
    )
    high = jnp.concatenate(
        [jnp.where(is_out, tail, nothing), jnp.where(is_out, nothing, tail)], axis=1
    ).astype(bf16)
    both = jnp.concatenate([low, high], axis=0)
    mine = dot(pick_ref[...], both, 0, 0)
    gates = gate_columns(gates_ref)
    out_ref[...] = (
        gates[:, 0:1] * mine[:rows, :width] + gates[:, 1:2] * mine[rows:, :width]
    ).astype(bf16)
    grad_ref[...] = (mine[:rows, width:] + mine[rows:, width:]).astype(bf16)


def combine(pick, gates, ret, rows):
    width = ret.shape[-1]
    shape = jax.ShapeDtypeStruct((rows, width), bf16)
    return pl.pallas_call(combine_kernel, out_shape=(shape, shape), name="combine")(
        pick, gates.T, ret
    )


def expert_kernel(core_ref, own_ref, other_ref, win_ref, wout_ref, mine_ref, theirs_ref, x_ref, s_ref, h_ref, d_ref, tail_ref, low_ref):
    n_y, experts, _, group, width = own_ref.shape
    core = core_ref[0]
    slots = experts * group
    half = slots // 2
    for y in range(n_y):
        for ref, which in ((own_ref, core), (other_ref, 1 - core)):
            at = pl.ds(pl.multiple_of((2 * y + which) * width, width), width)
            x_ref[0:slots, at] = ref[y, :, 0].reshape(slots, width)
            s_ref[0:slots, at] = ref[y, :, 1].reshape(slots, width)
            tail_ref[:, at] = ref[y, :, 2].reshape(slots, width)
    row = iota((half, slots), 0)
    source = iota((half, slots), 1)
    base = (row >> 2) * 8 + (row & 3)
    take_in = jnp.where(source == base, 1.0, 0.0).astype(bf16)
    take_scaled = jnp.where(source == base + 4, 1.0, 0.0).astype(bf16)
    tail = tail_ref[...]
    x_ref[slots : slots + half, :] = dot(take_in, tail).astype(bf16)
    s_ref[slots : slots + half, :] = dot(take_scaled, tail).astype(bf16)
    win = win_ref[...]
    wout = wout_ref[...]
    pre = dot(x_ref[...], win)
    cdf = 0.5 * (1.0 + lax.erf(pre * half_root))
    hidden = (pre * cdf).astype(bf16)
    h_ref[...] = hidden
    slope = cdf + pre * inv_root_tau * jnp.exp(-0.5 * pre * pre)
    d_pre = (dot(s_ref[...], wout, 1, 1) * slope).astype(bf16)
    d_ref[...] = d_pre
    out = dot(hidden, wout).astype(bf16)
    back = dot(d_pre, win, 1, 1).astype(bf16)
    low_ref[0] = out[0:slots]
    low_ref[1] = back[0:slots]
    tail_ref[...] = (dot(take_in, out[slots:], 0, 0) + dot(take_scaled, back[slots:], 0, 0)).astype(bf16)
    for y in range(n_y):
        for ref, which in ((mine_ref, core), (theirs_ref, 1 - core)):
            at = pl.ds(pl.multiple_of((2 * y + which) * width, width), width)
            ref[y, :, 0] = low_ref[0, :, at].reshape(experts, group, width)
            ref[y, :, 1] = low_ref[1, :, at].reshape(experts, group, width)
            ref[y, :, 2] = tail_ref[:, at].reshape(experts, group, width)


def expert_work(core, own, other, w_in, w_out):
    n_y, experts, _, group, width = own.shape
    slots = experts * group
    rows = slots + slots // 2
    model, units = w_in.shape
    part = jax.ShapeDtypeStruct(own.shape, bf16)
    vmem = pl.BlockSpec(memory_space=pltpu.VMEM)
    return pl.pallas_call(
        expert_kernel,
        in_specs=[pl.BlockSpec(memory_space=pltpu.SMEM)] + [vmem] * 4,
        out_specs=(vmem,) * 6,
        out_shape=(
            part,
            part,
            jax.ShapeDtypeStruct((rows, model), bf16),
            jax.ShapeDtypeStruct((rows, model), bf16),
            jax.ShapeDtypeStruct((rows, units), bf16),
            jax.ShapeDtypeStruct((rows, units), bf16),
        ),
        scratch_shapes=[pltpu.VMEM((slots, model), bf16), pltpu.VMEM((2, slots, model), bf16)],
        name="expert",
    )(core, own, other, w_in, w_out)


def on_device(tokens, cotangent, expert_ids, gate_weights, weight_in, weight_out):
    experts = lax.axis_size("x") * lax.axis_size("z")
    n_y = lax.axis_size("y")
    rows, width = tokens.shape
    swap = [(0, 1), (1, 0)]
    send, pick = dispatch(expert_ids, gate_weights, tokens, cotangent, experts)
    got = lax.all_to_all(send, XZ, 0, 0, tiled=True)
    own = lax.all_to_all(jnp.broadcast_to(got[None], (n_y,) + got.shape), "y", 0, 0, tiled=True)
    other = lax.ppermute(own, "core", swap)
    core = lax.axis_index("core").astype(jnp.int32).reshape(1)
    mine, theirs, x, s, h, d = expert_work(core, own, other, weight_in[0], weight_out[0])
    pair = (mine.astype(f32) + lax.ppermute(theirs, "core", swap).astype(f32)).astype(bf16)
    parts = lax.all_to_all(pair, "y", 0, 0, tiled=True)
    summed = jnp.sum(parts.astype(f32), axis=0).astype(bf16)
    ret = lax.all_to_all(summed, XZ, 0, 0, tiled=True)
    output, grad_tokens = combine(pick, gate_weights, ret, rows)
    grad_out = dot(h, s, 0, 0).astype(bf16)
    grad_in = dot(x, d, 0, 0).astype(bf16)
    return output, grad_tokens, grad_in[None], grad_out[None]


def solution(mesh):
    cores = 2
    n_dp, n_expert = mesh.devices.shape
    n_x = 4
    grid = mesh.devices.reshape(n_dp // cores, cores, n_x, n_expert // n_x)
    fine = Mesh(grid, ("y", "core", "x", "z"))
    dp = ("y", "core")
    return jax.shard_map(
        on_device,
        mesh=fine,
        in_specs=(P(XZ, dp), P(XZ, dp), P(XZ, None), P(XZ, None), P(XZ, None, dp), P(XZ, dp, None)),
        out_specs=(P(XZ, dp), P(XZ, dp), P(XZ, None, dp), P(XZ, dp, None)),
        check_vma=False,
    )
```

time: 204 us -> 159 us (0.78)
  waiting for transfers between devices: 51.5 us -> 27.2 us
  Pallas kernels: 0 us -> 16.5 us
  between operations: 14.4 us -> 0.7 us
  local copies, waits for them, and re-layouts: 13.3 us -> 2.14 us
  other arithmetic: 9.45 us -> 2.9 us
  matrix products: 11.4 us -> 5.25 us
  blocking collectives: 87.2 us -> 91.8 us
  starting transfers between devices: 15.9 us -> 12 us
    all_gather x1 -> x0, waiting for transfers between devices: 31.2 us -> none  [side_by_side(): lax.all_gather(both, axis, axis=dim, tiled=True)]
    pallas_call x0 -> x3, Pallas kernels: none -> 16.5 us  [the longest x1 11.3 us: expert_work(): pl.pallas_call(expert_kernel, in_specs=[pl.BlockSpec(memory_space=pltpu.S...]
    all_to_all x1, starting transfers between devices: 15.9 us -> 8.08 us  [on_device(): ret = lax.all_to_all(summed, XZ, 0, 0, tiled=True)]
    ppermute x0 -> x2, waiting for transfers between devices: none -> 6.83 us  [the longest x1 3.45 us: on_device(): lax.ppermute(theirs, 'core', swap).astype(f32)]
    dot_general x6 -> x2, matrix products: 11.4 us -> 5.25 us  [dot(): lax.dot_general(left, right, (((left_dim,), (right_dim,)), ((), ())), pre...]
    gather x6 -> x0, local copies, waits for them, and re-layouts: 5.92 us -> none  [the longest x2 1.93 us: on_device(): tokens[token_rows]]
    all_to_all x2 -> x3, blocking collectives: 87.2 us -> 91.8 us  [the longest x1 45.1 us: on_device(): got = lax.all_to_all(send, XZ, 0, 0, tiled=True)]
    ppermute x0 -> x2, starting transfers between devices: none -> 3.95 us  [the longest x1 2.04 us: on_device(): lax.ppermute(theirs, 'core', swap).astype(f32)]
  transfers between devices with their start and end apart: 2 -> 3, of which waited for: 2 -> 3; matrix products, arithmetic and copies ran while one was open for 3% -> 3% of each run, Pallas kernels for 0% -> 0%
where the time goes in v1:
time: 159 us; the launch traced here: 158 us
  blocking collectives  91.8 us (58%)
  waiting for transfers between devices  27.2 us (17%)
  Pallas kernels  16.5 us (10%)
  starting transfers between devices  12 us (8%)
  matrix products  5.25 us (3%)
  other arithmetic  2.9 us (2%)
  local copies, waits for them, and re-layouts  2.14 us (1%)
    all_to_all x1, blocking collectives, on_device(): got = lax.all_to_all(send, XZ, 0, 0, tiled=True)  45.1 us
    all_to_all x1, blocking collectives, on_device(): parts = lax.all_to_all(pair, 'y', 0, 0, tiled=True)  23.7 us
    all_to_all x1, blocking collectives, on_device(): lax.all_to_all(jnp.broadcast_to(got[None], (n_y,) + got.shape), 'y', 0, 0...  22.9 us
    all_to_all x1, waiting for transfers between devices, on_device(): ret = lax.all_to_all(summed, XZ, 0, 0, tiled=True)  20.4 us
    pallas_call x1, Pallas kernels, expert_work(): pl.pallas_call(expert_kernel, in_specs=[pl.BlockSpec(memory_space=pltpu.S...  11.3 us
    all_to_all x1, starting transfers between devices, on_device(): ret = lax.all_to_all(summed, XZ, 0, 0, tiled=True)  8.08 us
    dot_general x2, matrix products, dot(): lax.dot_general(left, right, (((left_dim,), (right_dim,)), ((), ())), pre...  5.25 us
    ppermute x1, waiting for transfers between devices, on_device(): lax.ppermute(theirs, 'core', swap).astype(f32)  3.45 us
  transfers between devices with their start and end apart: 3, of which 3 were waited for; matrix products, arithmetic and copies ran while one was open for 3% of the time, Pallas kernels for 0%

profile of v1, /device:TPU:6, one launch (start us, length us, event | category | flops | bytes accessed | tf_op | source)
XLA Modules:
  0.0 158.4 jit_solution(18417465181519427366)
XLA Ops:
  0.6 2.6 %dispatch.1 = (bf16[64,3,8,128]{3,2,1,0:T(8,128)(2,1)}, bf16[1024,512]{1,0:T(8,128)(2,1)}) custom-call(s32[2,256]{1,0:T(2,128)} %bitcast.17, f32[2,256]{1,0:T(2,128)} %bitcast.15, bf16[256,128]{1,0:T(8,128)(2,1)} %tok_ref.1, bf16[256,128]{1,0:T(8,128)(2,1)} %cot_ref.1), custom_call_target="tpu_custom_call" | custom-call | tf_op jit(solution)/shard_map/dispatch/pallas_call | solution.py:74
  3.3 45.1 %all_to_all.20 = bf16[64,3,8,128]{3,2,1,0:T(8,128)(2,1)S(1)} all-to-all(bf16[64,3,8,128]{3,2,1,0:T(8,128)(2,1)} %get-tuple-element.15), channel_id=1, replica_groups=mesh['y'=4,'core'=2,'x'=4,'z'=16] {'x','z'}, dimensions={0} | all-to-all | bytes 786432 | tf_op jit(solution)/shard_map/all_to_all | solution.py:186
  48.3 0.2 broadcast_in_dim.12
  48.5 22.9 %all_to_all.21.own_ref = bf16[4,64,3,8,128]{4,3,2,1,0:T(8,128)(2,1)S(1)} all-to-all(bf16[4,64,3,8,128]{4,3,2,1,0:T(8,128)(2,1)S(1)} %broadcast_in_dim.12), channel_id=1, replica_groups=mesh['y'=4,'core'=2,'x'=4,'z'=16] {'y'}, dimensions={0} | all-to-all | bytes 3145728 | tf_op jit(solution)/shard_map/all_to_all | solution.py:187
  71.5 0.0 copy-start
  71.5 1.9 %collective-permute-start = (bf16[4,64,3,8,128]{4,3,2,1,0:T(8,128)(2,1)S(1)}, bf16[4,64,3,8,128]{4,3,2,1,0:T(8,128)(2,1)S(1)}, u32[]{:S(2)}, u32[]{:S(2)}) collective-permute-start(bf16[4,64,3,8,128]{4,3,2,1,0:T(8,128)(2,1)S(1)} %all_to_all.21.own_ref), channel_id=1, source_target_pairs={{0,64},{64,0},{1,65},{65,1},{2,66},{66,2},{3,67},{67,3},{4,68},{68... | collective-permute-start | bytes 4718600 | tf_op jit(solution)/shard_map/ppermute | solution.py:188
  73.4 3.4 %collective-permute-done.other_ref = bf16[4,64,3,8,128]{4,3,2,1,0:T(8,128)(2,1)S(1)} collective-permute-done((bf16[4,64,3,8,128]{4,3,2,1,0:T(8,128)(2,1)S(1)}, bf16[4,64,3,8,128]{4,3,2,1,0:T(8,128)(2,1)S(1)}, u32[]{:S(2)}, u32[]{:S(2)}) %collective-permute-start) | collective-permute-done | bytes 1572896 | tf_op jit(solution)/shard_map/ppermute | solution.py:188
  76.8 0.0 copy-start.2
  76.8 0.0 copy-done
  76.8 1.2 copy-done.2
  77.9 11.3 %expert.1 = (bf16[4,64,3,8,128]{4,3,2,1,0:T(8,128)(2,1)}, bf16[4,64,3,8,128]{4,3,2,1,0:T(8,128)(2,1)}, bf16[768,1024]{1,0:T(8,128)(2,1)}, bf16[768,1024]{1,0:T(8...) custom-call(s32[1]{0:T(128)} %bitcast.2.core_ref, bf16[4,64,3,8,128]{4,3,2,1,0:T(8,128)(2,1)} %copy-done, ...), custom_call_target="tpu_custom_call" | custom-call | tf_op jit(solution)/shard_map/expert/pallas_call | solution.py:163
  89.3 2.0 %collective-permute-start.1 = (bf16[4,64,3,8,128]{4,3,2,1,0:T(8,128)(2,1)}, bf16[4,64,3,8,128]{4,3,2,1,0:T(8,128)(2,1)S(1)}, u32[]{:S(2)}, u32[]{:S(2)}) collective-permute-start(bf16[4,64,3,8,128]{4,3,2,1,0:T(8,128)(2,1)} %get-tuple-element.17), channel_id=1, source_target_pairs={{0,64},{64,0},{1,65},{65,1},{2,66},{66,2},{3,67},{67,3},{4,68},{68... | collective-permute-start | bytes 4718600 | tf_op jit(solution)/shard_map/ppermute | solution.py:191
  91.3 3.5 %collective-permute-done.1 = bf16[4,64,3,8,128]{4,3,2,1,0:T(8,128)(2,1)S(1)} collective-permute-done((bf16[4,64,3,8,128]{4,3,2,1,0:T(8,128)(2,1)}, bf16[4,64,3,8,128]{4,3,2,1,0:T(8,128)(2,1)S(1)}, u32[]{:S(2)}, u32[]{:S(2)}) %collective-permute-start.1) | collective-permute-done | bytes 1572896 | tf_op jit(solution)/shard_map/ppermute | solution.py:191
  94.8 1.8 %add_convert_fusion = bf16[4,64,3,8,128]{4,3,2,1,0:T(8,128)(2,1)S(1)} fusion(bf16[4,64,3,8,128]{4,3,2,1,0:T(8,128)(2,1)S(1)} %collective-permute-done.1, bf16[4,64,3,8,128]{4,3,2,1,0:T(8,128)(2,1)} %get-tuple-element.16), kind=kLoop, calls=%fused_computation | loop fusion | flops 3145728 | bytes 4718592 | tf_op jit(solution)/shard_map/convert_element_type | solution.py:191
  96.6 23.7 %all_to_all.22 = bf16[4,64,3,8,128]{4,3,2,1,0:T(8,128)(2,1)S(1)} all-to-all(bf16[4,64,3,8,128]{4,3,2,1,0:T(8,128)(2,1)S(1)} %add_convert_fusion), channel_id=1, replica_groups=mesh['y'=4,'core'=2,'x'=4,'z'=16] {'y'}, dimensions={0} | all-to-all | bytes 3145728 | tf_op jit(solution)/shard_map/all_to_all | solution.py:192
  120.3 0.0 copy-start.4
  120.3 1.1 reduce_sum.12
  121.4 8.1 %all-to-all-start.3 = ((bf16[64,3,8,128]{3,2,1,0:T(8,128)(2,1)}), bf16[64,3,8,128]{3,2,1,0:T(8,128)(2,1)S(1)}, u32[]{:S(2)}, u32[]{:S(2)}) async-start(bf16[64,3,8,128]{3,2,1,0:T(8,128)(2,1)} %reduce_sum.12), calls=%async_computation.3 | async-start | bytes 786432 | tf_op jit(solution)/shard_map/all_to_all | solution.py:194
  129.5 0.0 copy-done.4
  129.5 0.0 copy-start.3
  129.5 0.0 copy-start.5
  129.5 3.3 %fusion = bf16[1,1024,512]{2,1,0:T(8,128)(2,1)} fusion(bf16[768,1024]{1,0:T(8,128)(2,1)S(1)} %copy-done.4, bf16[768,512]{1,0:T(8,128)(2,1)} %get-tuple-element.21), kind=kOutput, calls=%fused_computation.3 | convolution fusion | flops 805830656 | bytes 3407872 | tf_op jit(solution)/shard_map/dot_general | solution.py:17
  132.8 0.0 copy-done.3
  132.8 0.0 copy-done.5
  132.8 2.0 %fusion.1 = bf16[1,512,1024]{2,1,0:T(8,128)(2,1)} fusion(bf16[768,512]{1,0:T(8,128)(2,1)S(1)} %copy-done.5, bf16[768,1024]{1,0:T(8,128)(2,1)S(1)} %copy-done.3), kind=kOutput, calls=%fused_computation.4 | convolution fusion | flops 805830656 | bytes 3407872 | tf_op jit(solution)/shard_map/dot_general | solution.py:17
  134.8 20.4 %all-to-all-done.3.ret_ref = bf16[64,3,8,128]{3,2,1,0:T(8,128)(2,1)S(1)} async-done(((bf16[64,3,8,128]{3,2,1,0:T(8,128)(2,1)}), bf16[64,3,8,128]{3,2,1,0:T(8,128)(2,1)S(1)}, u32[]{:S(2)}, u32[]{:S(2)}) %all-to-all-start.3) | async-done | bytes 393248 | tf_op jit(solution)/shard_map/all_to_all | solution.py:194
  155.1 0.0 copy-start.1
  155.2 0.7 copy-done.1
  155.9 2.5 %combine.1 = (bf16[256,128]{1,0:T(8,128)(2,1)}, bf16[256,128]{1,0:T(8,128)(2,1)}) custom-call(bf16[1024,512]{1,0:T(8,128)(2,1)} %get-tuple-element.14.pick_ref, f32[2,256]{1,0:T(2,128)} %bitcast.16, bf16[64,3,8,128]{3,2,1,0:T(8,128)(2,1)} %copy-done.1), custom_call_target="tpu_custom_call" | custom-call | tf_op jit(solution)/shard_map/combine/pallas_call | solution.py:110
Async XLA Ops:
  71.5 5.3 %copy-start = (bf16[4,64,3,8,128]{4,3,2,1,0:T(8,128)(2,1)}, bf16[4,64,3,8,128]{4,3,2,1,0:T(8,128)(2,1)S(1)}, u32[]{:S(2)}) copy-start(bf16[4,64,3,8,128]{4,3,2,1,0:T(8,128)(2,1)S(1)} %all_to_all.21.own_ref) | copy-start | bytes 4718596
  71.5 5.3 %collective-permute-start = (bf16[4,64,3,8,128]{4,3,2,1,0:T(8,128)(2,1)S(1)}, bf16[4,64,3,8,128]{4,3,2,1,0:T(8,128)(2,1)S(1)}, u32[]{:S(2)}, u32[]{:S(2)}) collective-permute-start(bf16[4,64,3,8,128]{4,3,2,1,0:T(8,128)(2,1)S(1)} %all_to_all.21.own_ref), channel_id=1, source_target_pairs={{0,64},{64,0},{1,65},{65,1},{2,66},{66,2},{3,67},{67,3},{4,68},{68... | collective-permute-start | bytes 4718600 | tf_op jit(solution)/shard_map/ppermute | solution.py:188
  76.8 1.2 copy-start.2
  89.3 5.5 %collective-permute-start.1 = (bf16[4,64,3,8,128]{4,3,2,1,0:T(8,128)(2,1)}, bf16[4,64,3,8,128]{4,3,2,1,0:T(8,128)(2,1)S(1)}, u32[]{:S(2)}, u32[]{:S(2)}) collective-permute-start(bf16[4,64,3,8,128]{4,3,2,1,0:T(8,128)(2,1)} %get-tuple-element.17), channel_id=1, source_target_pairs={{0,64},{64,0},{1,65},{65,1},{2,66},{66,2},{3,67},{67,3},{4,68},{68... | collective-permute-start | bytes 4718600 | tf_op jit(solution)/shard_map/ppermute | solution.py:191
  120.3 9.2 %copy-start.4 = (bf16[768,1024]{1,0:T(8,128)(2,1)S(1)}, bf16[768,1024]{1,0:T(8,128)(2,1)}, u32[]{:S(2)}) copy-start(bf16[768,1024]{1,0:T(8,128)(2,1)} %get-tuple-element.20) | copy-start | bytes 4718596
  121.4 33.7 %all-to-all-start.3 = ((bf16[64,3,8,128]{3,2,1,0:T(8,128)(2,1)}), bf16[64,3,8,128]{3,2,1,0:T(8,128)(2,1)S(1)}, u32[]{:S(2)}, u32[]{:S(2)}) async-start(bf16[64,3,8,128]{3,2,1,0:T(8,128)(2,1)} %reduce_sum.12), calls=%async_computation.3 | async-start | bytes 786432 | tf_op jit(solution)/shard_map/all_to_all | solution.py:194
  129.5 3.3 %copy-start.3 = (bf16[768,1024]{1,0:T(8,128)(2,1)S(1)}, bf16[768,1024]{1,0:T(8,128)(2,1)}, u32[]{:S(2)}) copy-start(bf16[768,1024]{1,0:T(8,128)(2,1)} %get-tuple-element.23) | copy-start | bytes 4718596
  129.5 3.3 %copy-start.5 = (bf16[768,512]{1,0:T(8,128)(2,1)S(1)}, bf16[768,512]{1,0:T(8,128)(2,1)}, u32[]{:S(2)}) copy-start(bf16[768,512]{1,0:T(8,128)(2,1)} %get-tuple-element.22) | copy-start | bytes 2359300
  155.1 0.7 copy-start.1

commit v2 on v1

v2 whole, which is shorter than its diff:
```python
import jax
import jax.numpy as jnp
from jax import lax
from jax.experimental import pallas as pl
from jax.experimental.pallas import tpu as pltpu
from jax.sharding import Mesh, PartitionSpec as P

half_root = 0.7071067811865476
inv_root_tau = 0.3989422804014327

XZ = ("x", "z")
bf16 = jnp.bfloat16
f32 = jnp.float32


def dot(left, right, left_dim=1, right_dim=0):
    return lax.dot_general(
        left, right, (((left_dim,), (right_dim,)), ((), ())), preferred_element_type=f32
    )


def iota(shape, dim):
    return lax.broadcasted_iota(jnp.int32, shape, dim)


def columns(rows):
    pad = jnp.zeros((8 - rows.shape[0], rows.shape[1]), rows.dtype)
    return jnp.transpose(jnp.concatenate([rows, pad], axis=0))


def ones_where(mask):
    return jnp.where(mask, 1.0, 0.0).astype(bf16)


def fetch(pairs, sems):
    copies = [pltpu.make_async_copy(src, dst, sems.at[i]) for i, (src, dst) in enumerate(pairs)]
    for copy in copies:
        copy.start()
    return copies


def dispatch_kernel(ids_hbm, gates_hbm, tok_hbm, cot_hbm, send_ref, ids_ref, gates_ref, tok_ref, cot_ref, sems):
    copies = fetch(
        ((ids_hbm, ids_ref), (gates_hbm, gates_ref), (tok_hbm, tok_ref), (cot_hbm, cot_ref)), sems
    )
    experts, _, group, width = send_ref.shape
    rows = tok_ref.shape[0]
    slots = experts * group
    which = iota((experts, rows), 0)
    earlier = ones_where(iota((rows, rows), 0) < iota((rows, rows), 1))
    at = iota((slots, experts), 0) - group * iota((slots, experts), 1)
    owner = ones_where((at >= 0) & (at < group))
    lane = iota((slots, 2 * rows), 0) & (group - 1)
    copies[0].wait()
    ids = ids_ref[...]
    first = which == ids[0:1, :]
    second = which == ids[1:2, :]
    rank = dot(ones_where(first | second), earlier)
    ranks = jnp.concatenate(
        [jnp.where(first, rank, -1.0), jnp.where(second, rank, -1.0)], axis=1
    ).astype(bf16)
    spread = dot(owner, ranks)
    low = ones_where(spread == lane.astype(f32))
    high = ones_where(spread == (8 + (lane & 3)).astype(f32))
    for copy in copies[1:]:
        copy.wait()
    gates = columns(gates_ref[...])
    cot = cot_ref[...].astype(f32)
    tok = tok_ref[...]
    source = jnp.concatenate(
        [
            jnp.concatenate([tok, (gates[:, 0:1] * cot).astype(bf16)], axis=1),
            jnp.concatenate([tok, (gates[:, 1:2] * cot).astype(bf16)], axis=1),
        ],
        axis=0,
    )
    chosen = dot(low, source).astype(bf16)
    rest = dot(high, source)
    mixed = jnp.where((iota((slots, width), 0) & 7) < 4, rest[:, :width], rest[:, width:])
    send_ref[:, 0] = chosen[:, :width].reshape(experts, group, width)
    send_ref[:, 1] = chosen[:, width:].reshape(experts, group, width)
    send_ref[:, 2] = mixed.astype(bf16).reshape(experts, group, width)


def dispatch(ids, gates, tokens, cotangent, experts):
    rows, width = tokens.shape
    return pl.pallas_call(
        dispatch_kernel,
        in_specs=[pl.BlockSpec(memory_space=pltpu.HBM)] * 4,
        out_shape=jax.ShapeDtypeStruct((experts, 3, 8, width), bf16),
        scratch_shapes=[
            pltpu.VMEM((2, rows), jnp.int32),
            pltpu.VMEM((2, rows), f32),
            pltpu.VMEM((rows, width), bf16),
            pltpu.VMEM((rows, width), bf16),
            pltpu.SemaphoreType.DMA((4,)),
        ],
        name="dispatch",
    )(ids.T, gates.T, tokens, cotangent)


def route_kernel(ids_ref, gates_ref, pick_ref, gate_ref):
    rows = ids_ref.shape[1]
    slots = pick_ref.shape[1] // 2
    experts = slots // 8
    ids = columns(ids_ref[...])
    which = iota((rows, experts), 1)
    first = which == ids[:, 0:1]
    second = which == ids[:, 1:2]
    earlier = ones_where(iota((rows, rows), 1) < iota((rows, rows), 0))
    rank = dot(earlier, ones_where(first | second))
    ranks = jnp.concatenate(
        [jnp.where(first, rank, -1.0), jnp.where(second, rank, -1.0)], axis=0
    ).astype(bf16)
    at = iota((experts, slots), 1) - 8 * iota((experts, slots), 0)
    spread = dot(ranks, ones_where((at >= 0) & (at < 8)))
    lane = iota((2 * rows, slots), 1) & 7
    pick_ref[:, 0:slots] = ones_where(spread == lane.astype(f32))
    pick_ref[:, slots : 2 * slots] = ones_where(spread == (8 + (lane & 3)).astype(f32))
    gates = columns(gates_ref[...])
    width = gate_ref.shape[1]
    gate_ref[0:rows, :] = jnp.broadcast_to(gates[:, 0:1], (rows, width))
    gate_ref[rows : 2 * rows, :] = jnp.broadcast_to(gates[:, 1:2], (rows, width))


def route(ids, gates, experts, width):
    rows = ids.shape[0]
    return pl.pallas_call(
        route_kernel,
        out_shape=(
            jax.ShapeDtypeStruct((2 * rows, experts * 16), bf16),
            jax.ShapeDtypeStruct((2 * rows, width), f32),
        ),
        compiler_params=pltpu.CompilerParams(vmem_limit_bytes=12 << 20),
        name="route",
    )(ids.T, gates.T)


def combine_kernel(pick_ref, gate_ref, ret_ref, out_ref, grad_ref):
    experts, _, group, width = ret_ref.shape
    rows = out_ref.shape[0]
    slots = experts * group
    tail = ret_ref[:, 2].reshape(slots, width).astype(f32)
    is_out = (iota((slots, width), 0) & 7) < 4
    low = jnp.concatenate(
        [ret_ref[:, 0].reshape(slots, width), ret_ref[:, 1].reshape(slots, width)], axis=1
    )
    high = jnp.concatenate(
        [jnp.where(is_out, tail, 0.0), jnp.where(is_out, 0.0, tail)], axis=1
    ).astype(bf16)
    mine = dot(pick_ref[...], jnp.concatenate([low, high], axis=0))
    scaled = gate_ref[...] * mine[:, :width]
    out_ref[...] = (scaled[:rows] + scaled[rows:]).astype(bf16)
    grad_ref[...] = (mine[:rows, width:] + mine[rows:, width:]).astype(bf16)


def combine(pick, gate, ret, rows):
    width = ret.shape[-1]
    shape = jax.ShapeDtypeStruct((rows, width), bf16)
    return pl.pallas_call(
        combine_kernel,
        out_shape=(shape, shape),
        compiler_params=pltpu.CompilerParams(vmem_limit_bytes=12 << 20),
        name="combine",
    )(pick, gate, ret)


def half_features(ref, out_ref):
    n_y, experts, _, group, width = ref.shape
    slots = experts * group
    half = slots // 2
    row, source = iota((half, slots), 0), iota((half, slots), 1)
    base = (row >> 2) * 8 + (row & 3)
    tails = []
    for y in range(n_y):
        at = slice(y * width, (y + 1) * width)
        out_ref[0, 0:slots, at] = ref[y, :, 0].reshape(slots, width)
        out_ref[1, 0:slots, at] = ref[y, :, 1].reshape(slots, width)
        tails.append(ref[y, :, 2].reshape(slots, width))
    tail = jnp.concatenate(tails, axis=1)
    out_ref[0, slots:, :] = dot(ones_where(source == base), tail).astype(bf16)
    out_ref[1, slots:, :] = dot(ones_where(source == base + 4), tail).astype(bf16)


def of_core(y, core, width):
    return pl.ds(pl.multiple_of((2 * y + core) * width, width), width)


def weight_copies(core, win_hbm, wout_hbm, win_ref, wout_ref, sems, n_y):
    width = win_ref.shape[0] // n_y
    pairs = []
    for y in range(n_y):
        at = of_core(y, core, width)
        here = pl.ds(y * width, width)
        pairs.append((win_hbm.at[at, :], win_ref.at[here, :]))
        pairs.append((wout_hbm.at[:, at], wout_ref.at[:, here]))
    return fetch(pairs, sems)


def own_kernel(core_ref, own_ref, win_hbm, wout_hbm, feat_ref, pre_ref, win_ref, wout_ref, sems):
    copies = weight_copies(core_ref[0], win_hbm, wout_hbm, win_ref, wout_ref, sems, own_ref.shape[0])
    half_features(own_ref, feat_ref)
    for copy in copies:
        copy.wait()
    pre_ref[0] = dot(feat_ref[0], win_ref[...])
    pre_ref[1] = dot(feat_ref[1], wout_ref[...], 1, 1)


def write_part(hidden, d_pre, win, wout, ref):
    n_y, experts, _, group, width = ref.shape
    slots = experts * group
    half = slots // 2
    row, source = iota((half, slots), 0), iota((half, slots), 1)
    base = (row >> 2) * 8 + (row & 3)
    out = dot(hidden, wout).astype(bf16)
    back = dot(d_pre, win, 1, 1).astype(bf16)
    tail = dot(ones_where(source == base), out[slots:], 0, 0)
    tail = (tail + dot(ones_where(source == base + 4), back[slots:], 0, 0)).astype(bf16)
    for y in range(n_y):
        at = slice(y * width, (y + 1) * width)
        ref[y, :, 0] = out[:slots, at].reshape(experts, group, width)
        ref[y, :, 1] = back[:slots, at].reshape(experts, group, width)
        ref[y, :, 2] = tail[:, at].reshape(experts, group, width)


def main_kernel(core_ref, other_ref, pre_ref, win_hbm, wout_hbm, theirs_ref, feat_ref, act_ref, win_ref, wout_ref, sems):
    copies = weight_copies(1 - core_ref[0], win_hbm, wout_hbm, win_ref, wout_ref, sems, other_ref.shape[0])
    half_features(other_ref, feat_ref)
    for copy in copies:
        copy.wait()
    win = win_ref[...]
    wout = wout_ref[...]
    pre = pre_ref[0] + dot(feat_ref[0], win)
    cdf = 0.5 * (1.0 + lax.erf(pre * half_root))
    hidden = (pre * cdf).astype(bf16)
    act_ref[0] = hidden
    slope = cdf + pre * inv_root_tau * jnp.exp(-0.5 * pre * pre)
    d_pre = ((pre_ref[1] + dot(feat_ref[1], wout, 1, 1)) * slope).astype(bf16)
    act_ref[1] = d_pre
    write_part(hidden, d_pre, win, wout, theirs_ref)


def mine_kernel(core_ref, own_ref, other_ref, act_ref, win_hbm, wout_hbm, mine_ref, feat_ref, win_ref, wout_ref, sems):
    core = core_ref[0]
    n_y = mine_ref.shape[0]
    width = mine_ref.shape[-1]
    copies = weight_copies(core, win_hbm, wout_hbm, win_ref, wout_ref, sems, n_y)
    for y in range(n_y):
        at = slice(y * width, (y + 1) * width)
        feat_ref[:, :, of_core(y, core, width)] = own_ref[:, :, at]
        feat_ref[:, :, of_core(y, 1 - core, width)] = other_ref[:, :, at]
    for copy in copies:
        copy.wait()
    write_part(act_ref[0], act_ref[1], win_ref[...], wout_ref[...], mine_ref)


def expert_call(kernel, name, operands, results, w_in, w_out):
    model, units = w_in.shape
    vmem = pl.BlockSpec(memory_space=pltpu.VMEM)
    weights = [pltpu.with_memory_space_constraint(w, pltpu.HBM) for w in (w_in, w_out)]
    return pl.pallas_call(
        kernel,
        in_specs=[pl.BlockSpec(memory_space=pltpu.SMEM)]
        + [vmem] * (len(operands) - 1)
        + [pl.BlockSpec(memory_space=pltpu.HBM)] * 2,
        out_specs=(vmem,) * len(results) if len(results) > 1 else vmem,
        out_shape=results if len(results) > 1 else results[0],
        scratch_shapes=[
            pltpu.VMEM((model // 2, units), bf16),
            pltpu.VMEM((units, model // 2), bf16),
            pltpu.SemaphoreType.DMA((8,)),
        ],
        compiler_params=pltpu.CompilerParams(vmem_limit_bytes=24 << 20),
        name=name,
    )(*operands, *weights)


def fold_kernel(parts_ref, out_ref):
    parts = [parts_ref[y].astype(f32) for y in range(parts_ref.shape[0])]
    out_ref[...] = sum(parts[1:], parts[0]).astype(bf16)


def fold(parts):
    return pl.pallas_call(
        fold_kernel,
        out_shape=jax.ShapeDtypeStruct(parts.shape[1:], bf16),
        compiler_params=pltpu.CompilerParams(vmem_limit_bytes=12 << 20),
        name="fold",
    )(parts)


def on_device(tokens, cotangent, expert_ids, gate_weights, weight_in, weight_out):
    experts = lax.axis_size("x") * lax.axis_size("z")
    n_y = lax.axis_size("y")
    rows, width = tokens.shape
    swap = [(0, 1), (1, 0)]
    send = dispatch(expert_ids, gate_weights, tokens, cotangent, experts)
    blocks = send.shape
    got = lax.all_to_all(send.reshape(experts, -1, width), XZ, 0, 0, tiled=True)
    got = jnp.broadcast_to(got.reshape(1, -1, width), (n_y, got.size // width, width))
    own = lax.all_to_all(got, "y", 0, 0, tiled=True)
    other = lax.ppermute(own, "core", swap).reshape((n_y,) + blocks)
    own = own.reshape((n_y,) + blocks)
    core = lax.axis_index("core").astype(jnp.int32).reshape(1)
    w_in, w_out = weight_in[0], weight_out[0]
    model, units = w_in.shape
    rows_in = experts * 12
    part = jax.ShapeDtypeStruct((n_y,) + blocks, bf16)
    feat = jax.ShapeDtypeStruct((2, rows_in, model // 2), bf16)
    act = jax.ShapeDtypeStruct((2, rows_in, units), bf16)
    own_feat, pre = expert_call(
        own_kernel,
        "own",
        (core, own),
        (feat, jax.ShapeDtypeStruct((2, rows_in, units), f32)),
        w_in,
        w_out,
    )
    theirs, other_feat, acts = expert_call(
        main_kernel, "main", (core, other, pre), (part, feat, act), w_in, w_out
    )
    mine, feats = expert_call(
        mine_kernel,
        "mine",
        (core, own_feat, other_feat, acts),
        (part, jax.ShapeDtypeStruct((2, rows_in, model), bf16)),
        w_in,
        w_out,
    )
    x, s, h, d = feats[0], feats[1], acts[0], acts[1]
    mine, theirs = (p.reshape(n_y, -1, width) for p in (mine, theirs))
    pair = (mine.astype(f32) + lax.ppermute(theirs, "core", swap).astype(f32)).astype(bf16)
    summed = fold(lax.all_to_all(pair, "y", 0, 0, tiled=True)).reshape(experts, -1, width)
    summed, ids, gates = lax.optimization_barrier((summed, expert_ids, gate_weights))
    pick, gate = route(ids, gates, experts, width)
    ret = lax.all_to_all(summed, XZ, 0, 0, tiled=True).reshape(blocks)
    output, grad_tokens = combine(pick, gate, ret, rows)
    grad_out = dot(h, s, 0, 0).astype(bf16)
    grad_in = dot(x, d, 0, 0).astype(bf16)
    return output, grad_tokens, grad_in[None], grad_out[None]


def solution(mesh):
    cores = 2
    n_dp, n_expert = mesh.devices.shape
    n_x = 4
    grid = mesh.devices.reshape(n_dp // cores, cores, n_x, n_expert // n_x)
    fine = Mesh(grid, ("y", "core", "x", "z"))
    dp = ("y", "core")
    return jax.shard_map(
        on_device,
        mesh=fine,
        in_specs=(P(XZ, dp), P(XZ, dp), P(XZ, None), P(XZ, None), P(XZ, None, dp), P(XZ, dp, None)),
        out_specs=(P(XZ, dp), P(XZ, dp), P(XZ, None, dp), P(XZ, dp, None)),
        check_vma=False,
    )
```

time: 159 us -> 148 us (0.931)
  waiting for transfers between devices: 27.2 us -> 19.9 us
  other arithmetic: 2.9 us -> 0.51 us
    ppermute x1, waiting for transfers between devices: 3.45 us -> 0.01 us  [on_device(): lax.ppermute(theirs, 'core', swap).astype(f32)]
    ppermute x1, waiting for transfers between devices: 3.37 us -> 0.55 us  [on_device(): other = lax.ppermute(own, 'core', swap).reshape((n_y,) + blocks)]
    pallas_call x3 -> x7, Pallas kernels: 16.5 us -> 15.7 us  [the longest x3 10.3 us: expert_call(): pl.pallas_call(kernel, in_specs=[pl.BlockSpec(memory_space=pltpu.SMEM)] +...]
  transfers between devices with their start and end apart: 3 -> 3, of which waited for: 3 -> 2; matrix products, arithmetic and copies ran while one was open for 3% -> 4% of each run, Pallas kernels for 0% -> 5%
where the time goes in v2:
time: 148 us
  blocking collectives  92 us (62%)
  waiting for transfers between devices  19.9 us (13%)
  Pallas kernels  15.7 us (11%)
  starting transfers between devices  12.1 us (8%)
  matrix products  5.53 us (4%)
    all_to_all x1, blocking collectives, on_device(): got = lax.all_to_all(send.reshape(experts, -1, width), XZ, 0, 0, tiled=True)  45.1 us
    all_to_all x1, blocking collectives, on_device(): lax.all_to_all(pair, 'y', 0, 0, tiled=True)  24 us
    all_to_all x1, blocking collectives, on_device(): own = lax.all_to_all(got, 'y', 0, 0, tiled=True)  22.9 us
    all_to_all x1, waiting for transfers between devices, on_device(): ret = lax.all_to_all(summed, XZ, 0, 0, tiled=True).reshape(blocks)  19.3 us
    pallas_call x3, Pallas kernels, expert_call(): pl.pallas_call(kernel, in_specs=[pl.BlockSpec(memory_space=pltpu.SMEM)] +...  10.3 us
    all_to_all x1, starting transfers between devices, on_device(): ret = lax.all_to_all(summed, XZ, 0, 0, tiled=True).reshape(blocks)  8.11 us
    dot_general x2, matrix products, dot(): lax.dot_general(left, right, (((left_dim,), (right_dim,)), ((), ())), pre...  5.53 us
  transfers between devices with their start and end apart: 3, of which 2 were waited for; matrix products, arithmetic and copies ran while one was open for 4% of the time, Pallas kernels for 5%

profile of v2, /device:TPU:6, one launch (start us, length us, event | category | flops | bytes accessed | tf_op | source)
XLA Modules:
  0.0 147.6 jit_solution(14782775311069220119)
XLA Ops:
  0.6 2.6 %dispatch.1 = bf16[64,3,8,128]{3,2,1,0:T(8,128)(2,1)} custom-call(s32[2,256]{1,0:T(2,128)} %bitcast.44, f32[2,256]{1,0:T(2,128)} %bitcast.46, bf16[256,128]{1,0:T(8,128)(2,1)} %tok_hbm.1, bf16[256,128]{1,0:T(8,128)(2,1)} %cot_hbm.1), custom_call_target="tpu_custom_call" | custom-call | tf_op jit(solution)/shard_map/dispatch/pallas_call | solution.py:87
  3.2 45.1 %all_to_all.20 = bf16[64,24,128]{2,1,0:T(8,128)(2,1)S(1)} all-to-all(bf16[64,24,128]{2,1,0:T(8,128)(2,1)} %bitcast.55), channel_id=1, replica_groups=mesh['y'=4,'core'=2,'x'=4,'z'=16] {'x','z'}, dimensions={0} | all-to-all | bytes 786432 | tf_op jit(solution)/shard_map/all_to_all | solution.py:299
  48.3 0.2 broadcast_in_dim.14
  48.5 22.9 %all_to_all.21 = bf16[4,1536,128]{2,1,0:T(8,128)(2,1)S(1)} all-to-all(bf16[4,1536,128]{2,1,0:T(8,128)(2,1)S(1)} %broadcast_in_dim.14), channel_id=1, replica_groups=mesh['y'=4,'core'=2,'x'=4,'z'=16] {'y'}, dimensions={0} | all-to-all | bytes 3145728 | tf_op jit(solution)/shard_map/all_to_all | solution.py:301
  71.4 1.9 %collective-permute-start = (bf16[4,1536,128]{2,1,0:T(8,128)(2,1)S(1)}, bf16[4,1536,128]{2,1,0:T(8,128)(2,1)S(1)}, u32[]{:S(2)}, u32[]{:S(2)}) collective-permute-start(bf16[4,1536,128]{2,1,0:T(8,128)(2,1)S(1)} %all_to_all.21), channel_id=1, source_target_pairs={{0,64},{64,0},{1,65},{65,1},{2,66},{66,2},{3,67},{67,3},{4,68},{68... | collective-permute-start | bytes 4718600 | tf_op jit(solution)/shard_map/ppermute | solution.py:302
  73.3 2.8 %own.1 = (bf16[2,768,512]{2,1,0:T(8,128)(2,1)S(1)}, f32[2,768,512]{2,1,0:T(8,128)S(1)}) custom-call(s32[1]{0:T(128)} %bitcast.core_ref, bf16[4,64,3,8,128]{4,3,2,1,0:T(8,128)(2,1)S(1)} %bitcast.41, bf16[1024,512]{1,0:T(8,128)(2,1)} %bitcast.49, bf16[512,1024]{1,0:T(8,128)(2,1)} %bitcast.52), custom_call_target="tpu_custom_call" | custom-call | tf_op jit(solution)/shard_map/own/pallas_call | solution.py:261
  76.1 0.5 collective-permute-done
  76.7 4.2 %main.1 = (bf16[4,64,3,8,128]{4,3,2,1,0:T(8,128)(2,1)S(1)}, bf16[2,768,512]{2,1,0:T(8,128)(2,1)S(1)}, bf16[2,768,512]{2,1,0:T(8,128)(2,1)S(1)}) custom-call(s32[1]{0:T(128)} %bitcast.core_ref, bf16[4,64,3,8,128]{4,3,2,1,0:T(8,128)(2,1)S(1)} %bitcast.42, f32[2,768,512]{2,1,0:T(8,128)S(1)} %get-tuple-element.19.pre_ref, bf16[1024,512]{1,0:T(8,128)(2,1)} %bitcast.50, ...), custom_call_target="tpu_custom_call" | custom-call | tf_op jit(solution)/shard_map/main/pallas_call | solution.py:261
  80.9 2.0 %collective-permute-start.1 = (bf16[4,1536,128]{2,1,0:T(8,128)(2,1)S(1)}, bf16[4,1536,128]{2,1,0:T(8,128)(2,1)S(1)}, u32[]{:S(2)}, u32[]{:S(2)}) collective-permute-start(bf16[4,1536,128]{2,1,0:T(8,128)(2,1)S(1)} %bitcast.48), channel_id=1, source_target_pairs={{0,64},{64,0},{1,65},{65,1},{2,66},{66,2},{3,67},{67,3},{4,68},{68... | collective-permute-start | bytes 4718600 | tf_op jit(solution)/shard_map/ppermute | solution.py:332
  82.9 3.3 %mine.1 = (bf16[4,64,3,8,128]{4,3,2,1,0:T(8,128)(2,1)S(1)}, bf16[2,768,1024]{2,1,0:T(8,128)(2,1)S(1)}) custom-call(s32[1]{0:T(128)} %bitcast.core_ref, bf16[2,768,512]{2,1,0:T(8,128)(2,1)S(1)} %get-tuple-element.18.own_ref, bf16[2,768,512]{2,1,0:T(8,128)(2,1)S(1)} %get-tuple-element.20.other_ref, bf16[2,768,512]{2,1,0:T(8,128)(2,1)S(1)} %get-tuple-element.21.act_ref, ...), custom_call_target="tpu_custom_call" | custom-call | tf_op jit(solution)/shard_map/mine/pallas_call | solution.py:261
  86.2 0.0 copy-start.2
  86.2 0.0 collective-permute-done.1
  86.2 0.5 fusion
  86.8 1.1 copy-done.2
  87.8 24.0 %all_to_all.22.parts_ref = bf16[4,1536,128]{2,1,0:T(8,128)(2,1)S(1)} all-to-all(bf16[4,1536,128]{2,1,0:T(8,128)(2,1)S(1)} %fusion), channel_id=1, replica_groups=mesh['y'=4,'core'=2,'x'=4,'z'=16] {'y'}, dimensions={0} | all-to-all | bytes 3145728 | tf_op jit(solution)/shard_map/all_to_all | solution.py:333
  111.8 0.9 fold.1
  112.8 8.1 %all-to-all-start.3 = ((bf16[64,24,128]{2,1,0:T(8,128)(2,1)}), bf16[64,24,128]{2,1,0:T(8,128)(2,1)S(1)}, u32[]{:S(2)}, u32[]{:S(2)}) async-start(bf16[64,24,128]{2,1,0:T(8,128)(2,1)} %bitcast.11), calls=%async_computation.3 | async-start | bytes 786432 | tf_op jit(solution)/shard_map/all_to_all | solution.py:336
  120.9 0.0 copy-start.3
  120.9 3.5 %fusion.13 = bf16[1,512,1024]{2,1,0:T(8,128)(2,1)} fusion(bf16[2,768,1024]{2,1,0:T(8,128)(2,1)} %copy-done.2, bf16[2,768,512]{2,1,0:T(8,128)(2,1)S(1)} %get-tuple-element.21.act_ref), kind=kOutput, calls=%fused_computation.10 | convolution fusion | flops 805830656 | bytes 3407872 | tf_op jit(solution)/shard_map/dot_general | solution.py:17
  124.4 0.0 copy-done.3
  124.4 0.0 copy-start
  124.4 0.0 copy-start.1
  124.4 2.0 %fusion.16 = bf16[1,1024,512]{2,1,0:T(8,128)(2,1)} fusion(bf16[2,768,1024]{2,1,0:T(8,128)(2,1)S(1)} %copy-done.3, bf16[2,768,512]{2,1,0:T(8,128)(2,1)S(1)} %get-tuple-element.21.act_ref), kind=kOutput, calls=%fused_computation.11 | convolution fusion | flops 805830656 | bytes 3407872 | tf_op jit(solution)/shard_map/dot_general | solution.py:17
  126.4 0.0 copy-done
  126.5 0.0 copy-done.1
  126.5 0.8 route.1
  127.2 19.3 %all-to-all-done.3 = bf16[64,24,128]{2,1,0:T(8,128)(2,1)S(1)} async-done(((bf16[64,24,128]{2,1,0:T(8,128)(2,1)}), bf16[64,24,128]{2,1,0:T(8,128)(2,1)S(1)}, u32[]{:S(2)}, u32[]{:S(2)}) %all-to-all-start.3) | async-done | bytes 393248 | tf_op jit(solution)/shard_map/all_to_all | solution.py:336
  146.5 1.1 combine.1
Async XLA Ops:
  71.4 5.3 %collective-permute-start = (bf16[4,1536,128]{2,1,0:T(8,128)(2,1)S(1)}, bf16[4,1536,128]{2,1,0:T(8,128)(2,1)S(1)}, u32[]{:S(2)}, u32[]{:S(2)}) collective-permute-start(bf16[4,1536,128]{2,1,0:T(8,128)(2,1)S(1)} %all_to_all.21), channel_id=1, source_target_pairs={{0,64},{64,0},{1,65},{65,1},{2,66},{66,2},{3,67},{67,3},{4,68},{68... | collective-permute-start | bytes 4718600 | tf_op jit(solution)/shard_map/ppermute | solution.py:302
  80.9 5.3 %collective-permute-start.1 = (bf16[4,1536,128]{2,1,0:T(8,128)(2,1)S(1)}, bf16[4,1536,128]{2,1,0:T(8,128)(2,1)S(1)}, u32[]{:S(2)}, u32[]{:S(2)}) collective-permute-start(bf16[4,1536,128]{2,1,0:T(8,128)(2,1)S(1)} %bitcast.48), channel_id=1, source_target_pairs={{0,64},{64,0},{1,65},{65,1},{2,66},{66,2},{3,67},{67,3},{4,68},{68... | collective-permute-start | bytes 4718600 | tf_op jit(solution)/shard_map/ppermute | solution.py:332
  86.2 1.6 %copy-start.2 = (bf16[2,768,1024]{2,1,0:T(8,128)(2,1)}, bf16[2,768,1024]{2,1,0:T(8,128)(2,1)S(1)}, u32[]{:S(2)}) copy-start(bf16[2,768,1024]{2,1,0:T(8,128)(2,1)S(1)} %get-tuple-element.31) | copy-start | bytes 9437188
  112.8 33.8 %all-to-all-start.3 = ((bf16[64,24,128]{2,1,0:T(8,128)(2,1)}), bf16[64,24,128]{2,1,0:T(8,128)(2,1)S(1)}, u32[]{:S(2)}, u32[]{:S(2)}) async-start(bf16[64,24,128]{2,1,0:T(8,128)(2,1)} %bitcast.11), calls=%async_computation.3 | async-start | bytes 786432 | tf_op jit(solution)/shard_map/all_to_all | solution.py:336
  120.9 3.5 %copy-start.3 = (bf16[2,768,1024]{2,1,0:T(8,128)(2,1)S(1)}, bf16[2,768,1024]{2,1,0:T(8,128)(2,1)}, u32[]{:S(2)}) copy-start(bf16[2,768,1024]{2,1,0:T(8,128)(2,1)} %copy-done.2) | copy-start | bytes 9437188
  124.4 2.0 %copy-start = (s32[256,2]{0,1:T(2,128)S(1)}, s32[256,2]{0,1:T(2,128)}, u32[]{:S(2)}) copy-start(s32[256,2]{0,1:T(2,128)} %param.8) | copy-start | bytes 6148
  124.4 2.0 %copy-start.1 = (f32[256,2]{0,1:T(2,128)S(1)}, f32[256,2]{0,1:T(2,128)}, u32[]{:S(2)}) copy-start(f32[256,2]{0,1:T(2,128)} %param.9) | copy-start | bytes 6148

commit v3 on v2

v3 whole, which is shorter than its diff:
```python
import jax
import jax.numpy as jnp
from jax import lax
from jax.experimental import pallas as pl
from jax.experimental.pallas import tpu as pltpu
from jax.sharding import Mesh, PartitionSpec as P

half_root = 0.7071067811865476
inv_root_tau = 0.3989422804014327

XZ = ("x", "z")
CXZ = ("core", "x", "z")
bf16 = jnp.bfloat16
f32 = jnp.float32

HALF = 6
CHUNK = 12


def dot(left, right, left_dim=1, right_dim=0):
    return lax.dot_general(
        left, right, (((left_dim,), (right_dim,)), ((), ())), preferred_element_type=f32
    )


def iota(shape, dim):
    return lax.broadcasted_iota(jnp.int32, shape, dim)


def columns(rows):
    pad = jnp.zeros((8 - rows.shape[0], rows.shape[1]), rows.dtype)
    return jnp.transpose(jnp.concatenate([rows, pad], axis=0))


def ones_where(mask):
    return jnp.where(mask, 1.0, 0.0).astype(bf16)


def fetch(pairs, sems):
    copies = [pltpu.make_async_copy(src, dst, sems.at[i]) for i, (src, dst) in enumerate(pairs)]
    for copy in copies:
        copy.start()
    return copies


def row_of(shape, dim, experts):
    row = iota(shape, dim)
    chunk = ((row.astype(f32) + 0.5) * (1.0 / CHUNK)).astype(jnp.int32)
    at = row - CHUNK * chunk
    core = jnp.where(chunk >= experts, 1, 0)
    group, place = at >> 2, at & 3
    mixed = group == 1
    is_input = jnp.where(mixed, place >> 1, group) == 0
    slot = HALF * core + jnp.where(mixed, 4 + (place & 1), place)
    return chunk - experts * core, slot, is_input


def dispatch_kernel(ids_hbm, gates_hbm, tok_hbm, cot_hbm, send_ref, ids_ref, gates_ref, tok_ref, cot_ref, sems):
    copies = fetch(
        ((ids_hbm, ids_ref), (gates_hbm, gates_ref), (tok_hbm, tok_ref), (cot_hbm, cot_ref)), sems
    )
    n_send, width = send_ref.shape
    experts = n_send // (2 * CHUNK)
    rows = tok_ref.shape[0]
    which = iota((experts, rows), 0)
    earlier = ones_where(iota((rows, rows), 0) < iota((rows, rows), 1))
    expert, slot, is_input = row_of((n_send, 1), 0, experts)
    owner = ones_where(expert == iota((n_send, experts), 1))
    copies[0].wait()
    ids = ids_ref[...]
    first = which == ids[0:1, :]
    second = which == ids[1:2, :]
    rank = dot(ones_where(first | second), earlier)
    ranks = jnp.concatenate(
        [jnp.where(first, rank, -1.0), jnp.where(second, rank, -1.0)], axis=1
    ).astype(bf16)
    pick = ones_where(dot(owner, ranks) == slot.astype(f32))
    for copy in copies[1:]:
        copy.wait()
    gates = columns(gates_ref[...])
    cot = cot_ref[...].astype(f32)
    tok = tok_ref[...]
    source = jnp.concatenate(
        [
            jnp.concatenate([tok, (gates[:, 0:1] * cot).astype(bf16)], axis=1),
            jnp.concatenate([tok, (gates[:, 1:2] * cot).astype(bf16)], axis=1),
        ],
        axis=0,
    )
    both = dot(pick, source)
    send_ref[...] = jnp.where(is_input, both[:, :width], both[:, width:]).astype(bf16)


def in_hbm(*arrays):
    return [pltpu.with_memory_space_constraint(a, pltpu.HBM) for a in arrays]


def dispatch(ids, gates, tokens, cotangent, experts):
    rows, width = tokens.shape
    return pl.pallas_call(
        dispatch_kernel,
        in_specs=[pl.BlockSpec(memory_space=pltpu.HBM)] * 4,
        out_shape=jax.ShapeDtypeStruct((2 * experts * CHUNK, width), bf16),
        scratch_shapes=[
            pltpu.VMEM((2, rows), jnp.int32),
            pltpu.VMEM((2, rows), f32),
            pltpu.VMEM((rows, width), bf16),
            pltpu.VMEM((rows, width), bf16),
            pltpu.SemaphoreType.DMA((4,)),
        ],
        compiler_params=pltpu.CompilerParams(vmem_limit_bytes=16 << 20),
        name="dispatch",
    )(*in_hbm(ids.T, gates.T, tokens, cotangent))


def route_kernel(ids_ref, gates_ref, pick_ref, gate_ref):
    rows = ids_ref.shape[1]
    n_send = pick_ref.shape[1]
    experts = n_send // (2 * CHUNK)
    ids = columns(ids_ref[...])
    which = iota((rows, experts), 1)
    first = which == ids[:, 0:1]
    second = which == ids[:, 1:2]
    earlier = ones_where(iota((rows, rows), 1) < iota((rows, rows), 0))
    rank = dot(earlier, ones_where(first | second))
    ranks = jnp.concatenate(
        [jnp.where(first, rank, -1.0), jnp.where(second, rank, -1.0)], axis=0
    ).astype(bf16)
    expert, slot, _ = row_of((1, n_send), 1, experts)
    owner = ones_where(expert == iota((experts, n_send), 0))
    pick_ref[...] = ones_where(dot(ranks, owner) == slot.astype(f32))
    gates = columns(gates_ref[...])
    width = gate_ref.shape[1]
    gate_ref[0:rows, :] = jnp.broadcast_to(gates[:, 0:1], (rows, width))
    gate_ref[rows : 2 * rows, :] = jnp.broadcast_to(gates[:, 1:2], (rows, width))


def route(ids, gates, experts, width):
    rows = ids.shape[0]
    return pl.pallas_call(
        route_kernel,
        out_shape=(
            jax.ShapeDtypeStruct((2 * rows, 2 * experts * CHUNK), bf16),
            jax.ShapeDtypeStruct((2 * rows, width), f32),
        ),
        compiler_params=pltpu.CompilerParams(vmem_limit_bytes=16 << 20),
        name="route",
    )(ids.T, gates.T)


def combine_kernel(pick_ref, gate_ref, ret_ref, out_ref, grad_ref):
    n_send, width = ret_ref.shape
    rows = out_ref.shape[0]
    _, _, is_out = row_of((n_send, 1), 0, n_send // (2 * CHUNK))
    ret = ret_ref[...].astype(f32)
    both = jnp.concatenate(
        [jnp.where(is_out, ret, 0.0), jnp.where(is_out, 0.0, ret)], axis=1
    ).astype(bf16)
    mine = dot(pick_ref[...], both)
    scaled = gate_ref[...] * mine[:, :width]
    out_ref[...] = (scaled[:rows] + scaled[rows:]).astype(bf16)
    grad_ref[...] = (mine[:rows, width:] + mine[rows:, width:]).astype(bf16)


def combine(pick, gate, ret, rows):
    width = ret.shape[-1]
    shape = jax.ShapeDtypeStruct((rows, width), bf16)
    return pl.pallas_call(
        combine_kernel,
        out_shape=(shape, shape),
        compiler_params=pltpu.CompilerParams(vmem_limit_bytes=16 << 20),
        name="combine",
    )(pick, gate, ret)


def expert_kernel(got_ref, win0, wout0, win1, wout1, part_ref, x_hbm, s_hbm, h_hbm, d_hbm, win_ref, wout_ref, x_ref, s_ref, h_ref, d_ref, sems):
    weights = fetch(
        (
            (win0, win_ref.at[0]),
            (win1, win_ref.at[1]),
            (wout0, wout_ref.at[0]),
            (wout1, wout_ref.at[1]),
        ),
        sems,
    )
    n_y, n_rows, width = got_ref.shape
    group = n_rows // 3
    full = group // 2
    half = full // 2
    row, source = iota((half, full), 0), iota((half, full), 1)
    base = (row >> 1) * 4 + (row & 1)
    take_in = ones_where(source == base)
    take_scaled = ones_where(source == base + 2)
    tails = []
    for y in range(n_y):
        for c in range(2):
            at = slice((2 * y + c) * width, (2 * y + c + 1) * width)
            x_ref[0:full, at] = got_ref[y, c * full : (c + 1) * full]
            s_ref[0:full, at] = got_ref[y, 2 * group + c * full : 2 * group + (c + 1) * full]
            tails.append(got_ref[y, group + c * full : group + (c + 1) * full])
    tail = jnp.concatenate(tails, axis=1)
    x_ref[full:, :] = dot(take_in, tail).astype(bf16)
    s_ref[full:, :] = dot(take_scaled, tail).astype(bf16)
    saves = [pltpu.make_async_copy(x_ref, x_hbm, sems.at[4])]
    saves.append(pltpu.make_async_copy(s_ref, s_hbm, sems.at[5]))
    for save in saves:
        save.start()
    out = back = None
    for c in range(2):
        weights[c].wait()
        pre = dot(x_ref[...], win_ref[c])
        cdf = 0.5 * (1.0 + lax.erf(pre * half_root))
        hidden = (pre * cdf).astype(bf16)
        h_ref[c] = hidden
        slope = cdf + pre * inv_root_tau * jnp.exp(-0.5 * pre * pre)
        weights[2 + c].wait()
        d_pre = (dot(s_ref[...], wout_ref[c], 1, 1) * slope).astype(bf16)
        d_ref[c] = d_pre
        for save in (
            pltpu.make_async_copy(h_ref.at[c], h_hbm.at[c], sems.at[6 + c]),
            pltpu.make_async_copy(d_ref.at[c], d_hbm.at[c], sems.at[8 + c]),
        ):
            save.start()
            saves.append(save)
        more, less = dot(hidden, wout_ref[c]), dot(d_pre, win_ref[c], 1, 1)
        out, back = (more, less) if c == 0 else (out + more, back + less)
    out, back = out.astype(bf16), back.astype(bf16)
    tail = dot(take_in, out[full:], 0, 0) + dot(take_scaled, back[full:], 0, 0)
    tail = tail.astype(bf16)
    for y in range(n_y):
        for c in range(2):
            at = slice((2 * y + c) * width, (2 * y + c + 1) * width)
            for k, block in enumerate((out, tail, back)):
                to = k * group + c * full
                part_ref[y, to : to + full] = block[:full, at]
    for save in saves:
        save.wait()


def expert_work(got, w_in, w_out, other_in, other_out):
    n_y, n_rows, width = got.shape
    model, units = w_in.shape
    rows = n_rows // 4
    hbm = pl.BlockSpec(memory_space=pltpu.HBM)
    vmem = pl.BlockSpec(memory_space=pltpu.VMEM)
    feats = pltpu.HBM((rows, model), bf16)
    acts = pltpu.HBM((2, rows, units), bf16)
    return pl.pallas_call(
        expert_kernel,
        in_specs=[vmem] + [hbm] * 4,
        out_specs=[vmem] + [hbm] * 4,
        out_shape=(jax.ShapeDtypeStruct(got.shape, bf16), feats, feats, acts, acts),
        scratch_shapes=[
            pltpu.VMEM((2, model, units), bf16),
            pltpu.VMEM((2, units, model), bf16),
            pltpu.VMEM((rows, model), bf16),
            pltpu.VMEM((rows, model), bf16),
            pltpu.VMEM((2, rows, units), bf16),
            pltpu.VMEM((2, rows, units), bf16),
            pltpu.SemaphoreType.DMA((10,)),
        ],
        compiler_params=pltpu.CompilerParams(vmem_limit_bytes=32 << 20),
        name="expert",
    )(got, *in_hbm(w_in, w_out, other_in, other_out))


def fold_kernel(parts_ref, out_ref):
    parts = [parts_ref[y].astype(f32) for y in range(parts_ref.shape[0])]
    out_ref[...] = sum(parts[1:], parts[0]).astype(bf16)


def fold(parts):
    return pl.pallas_call(
        fold_kernel,
        out_shape=jax.ShapeDtypeStruct(parts.shape[1:], bf16),
        compiler_params=pltpu.CompilerParams(vmem_limit_bytes=12 << 20),
        name="fold",
    )(parts)


def on_device(tokens, cotangent, expert_ids, gate_weights, weight_in, weight_out):
    experts = lax.axis_size("x") * lax.axis_size("z")
    n_y = lax.axis_size("y")
    rows, width = tokens.shape
    swap = [(0, 1), (1, 0)]
    w_in, w_out = weight_in[0], weight_out[0]
    send = dispatch(expert_ids, gate_weights, tokens, cotangent, experts)
    chunks = (2 * experts, CHUNK // 4, 4, width)
    with jax.named_scope("to_experts"):
        got = lax.all_to_all(send.reshape(chunks), CXZ, 0, 0, tiled=True)
    with jax.named_scope("weights"):
        other_in = lax.ppermute(w_in, "core", swap)
        other_out = lax.ppermute(w_out, "core", swap)
    got = jnp.transpose(got, (1, 0, 2, 3)).reshape(1, -1, width)
    got = jnp.broadcast_to(got, (n_y,) + got.shape[1:])
    got = lax.all_to_all(got, "y", 0, 0, tiled=True)
    part, x, s, h, d = expert_work(got, w_in, w_out, other_in, other_out)
    summed = fold(lax.all_to_all(part, "y", 0, 0, tiled=True))
    summed = jnp.transpose(summed.reshape(chunks[1], chunks[0], 4, width), (1, 0, 2, 3))
    summed, ids, gates = lax.optimization_barrier((summed, expert_ids, gate_weights))
    pick, gate = route(ids, gates, experts, width)
    ret = lax.all_to_all(summed, CXZ, 0, 0, tiled=True).reshape(-1, width)
    output, grad_tokens = combine(pick, gate, ret, rows)
    their_out = lax.ppermute(dot(h[1], s, 0, 0).astype(bf16), "core", swap)
    their_in = lax.ppermute(dot(x, d[1], 0, 0).astype(bf16), "core", swap)
    grad_out = (dot(h[0], s, 0, 0) + their_out.astype(f32)).astype(bf16)
    grad_in = (dot(x, d[0], 0, 0) + their_in.astype(f32)).astype(bf16)
    return output, grad_tokens, grad_in[None], grad_out[None]


def solution(mesh):
    cores = 2
    n_dp, n_expert = mesh.devices.shape
    n_x = 4
    grid = mesh.devices.reshape(n_dp // cores, cores, n_x, n_expert // n_x)
    fine = Mesh(grid, ("y", "core", "x", "z"))
    dp = ("y", "core")
    return jax.shard_map(
        on_device,
        mesh=fine,
        in_specs=(P(XZ, dp), P(XZ, dp), P(XZ, None), P(XZ, None), P(XZ, None, dp), P(XZ, dp, None)),
        out_specs=(P(XZ, dp), P(XZ, dp), P(XZ, None, dp), P(XZ, dp, None)),
        check_vma=False,
    )
```

time: 148 us -> 146 us (0.986); the launches traced: 148 us -> 143 us
  blocking collectives: 92 us -> 44.1 us
  waiting for transfers between devices: 19.9 us -> 48.3 us
  starting transfers between devices: 12.1 us -> 25.6 us
  Pallas kernels: 15.7 us -> 13 us
  matrix products: 5.53 us -> 8.1 us
  local copies, waits for them, and re-layouts: 1.3 us -> 3.4 us
    all_to_all x3 -> x1, blocking collectives: 92 us -> 44.1 us  [on_device(): got = lax.all_to_all(send.reshape(chunks), CXZ, 0, 0, tiled=True)]
    all_to_all x1 -> x3, waiting for transfers between devices: 19.3 us -> 45.8 us  [the longest x1 16.4 us: on_device(): summed = fold(lax.all_to_all(part, 'y', 0, 0, tiled=True))]
    all_to_all x1 -> x3, starting transfers between devices: 8.11 us -> 16.6 us  [the longest x1 8.3 us: on_device(): ret = lax.all_to_all(summed, CXZ, 0, 0, tiled=True).reshape(-1, width)]
    ppermute x2 -> x4, starting transfers between devices: 3.95 us -> 9.04 us  [the longest x1 2.61 us: on_device(): other_in = lax.ppermute(w_in, 'core', swap)]
    dot_general x2 -> x4, matrix products: 5.53 us -> 8.1 us  [dot(): lax.dot_general(left, right, (((left_dim,), (right_dim,)), ((), ())), pre...]
    pallas_call x4 -> x2, Pallas kernels: 11 us -> 8.99 us  [the longest x1 7.9 us: expert_work(): pl.pallas_call(expert_kernel, in_specs=[vmem] + [hbm] * 4, out_specs=[vme...]
    ppermute x2 -> x4, waiting for transfers between devices: 0.55 us -> 2.52 us  [the longest x1 1.66 us: on_device(): other_out = lax.ppermute(w_out, 'core', swap)]
  transfers between devices with their start and end apart: 3 -> 7, of which waited for: 2 -> 6; matrix products, arithmetic and copies ran while one was open for 4% -> 6% of each run, Pallas kernels for 5% -> 1%
where the time goes in v3:
time: 146 us; the launch traced here: 143 us
  waiting for transfers between devices  48.3 us (33%)
  blocking collectives  44.1 us (30%)
  starting transfers between devices  25.6 us (18%)
  Pallas kernels  13 us (9%)
  matrix products  8.1 us (6%)
  local copies, waits for them, and re-layouts  3.4 us (2%)
    all_to_all x1, blocking collectives, on_device(): got = lax.all_to_all(send.reshape(chunks), CXZ, 0, 0, tiled=True)  44.1 us
    all_to_all x1, waiting for transfers between devices, on_device(): summed = fold(lax.all_to_all(part, 'y', 0, 0, tiled=True))  16.4 us
    all_to_all x1, waiting for transfers between devices, on_device(): ret = lax.all_to_all(summed, CXZ, 0, 0, tiled=True).reshape(-1, width)  15.1 us
    all_to_all x1, waiting for transfers between devices, on_device(): got = lax.all_to_all(got, 'y', 0, 0, tiled=True)  14.3 us
    all_to_all x1, starting transfers between devices, on_device(): ret = lax.all_to_all(summed, CXZ, 0, 0, tiled=True).reshape(-1, width)  8.3 us
    dot_general x4, matrix products, dot(): lax.dot_general(left, right, (((left_dim,), (right_dim,)), ((), ())), pre...  8.1 us
    pallas_call x1, Pallas kernels, expert_work(): pl.pallas_call(expert_kernel, in_specs=[vmem] + [hbm] * 4, out_specs=[vme...  7.9 us
    all_to_all x1, starting transfers between devices, on_device(): got = lax.all_to_all(got, 'y', 0, 0, tiled=True)  4.6 us
  transfers between devices with their start and end apart: 7, of which 6 were waited for; matrix products, arithmetic and copies ran while one was open for 6% of the time, Pallas kernels for 1%

profile of v3, /device:TPU:6, one launch (start us, length us, event | category | flops | bytes accessed | tf_op | source)
XLA Modules:
  0.0 143.3 jit_solution(12992315449039489010)
XLA Ops:
  0.6 2.5 %dispatch.1 = bf16[1536,128]{1,0:T(8,128)(2,1)S(1)} custom-call(s32[2,256]{1,0:T(2,128)} %bitcast.37, f32[2,256]{1,0:T(2,128)} %bitcast.39, bf16[256,128]{1,0:T(8,128)(2,1)} %tok_hbm.1, bf16[256,128]{1,0:T(8,128)(2,1)} %cot_hbm.1), custom_call_target="tpu_custom_call" | custom-call | tf_op jit(solution)/shard_map/dispatch/pallas_call | solution.py:100
  3.2 44.1 %all_to_all.20 = bf16[128,3,4,128]{3,2,1,0:T(4,128)(2,1)S(1)} all-to-all(bf16[128,3,4,128]{3,2,1,0:T(4,128)(2,1)S(1)} %bitcast.34), channel_id=1, replica_groups=mesh['y'=4,'core'=2,'x'=4,'z'=16] {'core','x','z'}, dimensions={0} | all-to-all | bytes 786432 | tf_op jit(solution)/shard_map/to_experts/all_to_all | solution.py:290
  47.3 0.1 copy.10
  47.4 1.4 broadcast_in_dim.14
  48.8 0.0 copy-start.2
  48.8 4.6 %all-to-all-start.1 = ((bf16[4,1536,128]{2,1,0:T(8,128)(2,1)}), bf16[4,1536,128]{2,1,0:T(8,128)(2,1)S(1)}, u32[]{:S(2)}, u32[]{:S(2)}) async-start(bf16[4,1536,128]{2,1,0:T(8,128)(2,1)} %broadcast_in_dim.14), calls=%async_computation.1 | async-start | bytes 3145728 | tf_op jit(solution)/shard_map/all_to_all | solution.py:296
  53.4 0.0 copy-done.2
  53.4 2.6 %collective-permute-start = (bf16[1024,512]{1,0:T(8,128)(2,1)S(1)}, bf16[1024,512]{1,0:T(8,128)(2,1)S(1)}, u32[]{:S(2)}, u32[]{:S(2)}) collective-permute-start(bf16[1024,512]{1,0:T(8,128)(2,1)S(1)} %bitcast.44), channel_id=1, source_target_pairs={{0,64},{64,0},{1,65},{65,1},{2,66},{66,2},{3,67},{67,3},{4,68},{68... | collective-permute-start | bytes 3145736 | tf_op jit(solution)/shard_map/weights/ppermute | solution.py:292
  56.0 1.9 %collective-permute-start.1 = (bf16[512,1024]{1,0:T(8,128)(2,1)}, bf16[512,1024]{1,0:T(8,128)(2,1)}, u32[]{:S(2)}, u32[]{:S(2)}) collective-permute-start(bf16[512,1024]{1,0:T(8,128)(2,1)} %bitcast.45), channel_id=1, source_target_pairs={{0,64},{64,0},{1,65},{65,1},{2,66},{66,2},{3,67},{67,3},{4,68},{68... | collective-permute-start | bytes 3145736 | tf_op jit(solution)/shard_map/weights/ppermute | solution.py:293
  57.9 0.3 collective-permute-done.win1
  58.3 0.0 copy-start.3
  58.3 1.0 copy-done.3
  59.2 1.7 %collective-permute-done.1.wout1 = bf16[512,1024]{1,0:T(8,128)(2,1)} collective-permute-done((bf16[512,1024]{1,0:T(8,128)(2,1)}, bf16[512,1024]{1,0:T(8,128)(2,1)}, u32[]{:S(2)}, u32[]{:S(2)}) %collective-permute-start.1) | collective-permute-done | bytes 1048608 | tf_op jit(solution)/shard_map/weights/ppermute | solution.py:293
  60.9 14.3 %all-to-all-done.1.got_ref = bf16[4,1536,128]{2,1,0:T(8,128)(2,1)S(1)} async-done(((bf16[4,1536,128]{2,1,0:T(8,128)(2,1)}), bf16[4,1536,128]{2,1,0:T(8,128)(2,1)S(1)}, u32[]{:S(2)}, u32[]{:S(2)}) %all-to-all-start.1) | async-done | bytes 1572896 | tf_op jit(solution)/shard_map/all_to_all | solution.py:296
  75.3 7.9 %expert.1 = (bf16[4,1536,128]{2,1,0:T(8,128)(2,1)}, bf16[384,1024]{1,0:T(8,128)(2,1)}, bf16[384,1024]{1,0:T(8,128)(2,1)}, bf16[2,384,512]{2,1,0:T(8,128)(2,1)}, bf16[2,384,512]{2,1,0:T(8,128)(2,1)}) custom-call(bf16[4,1536,128]{2,1,0:T(8,128)(2,1)S(1)} %all-to-all-done.1.got_ref, bf16[1024,512]{1,0:T(8,128)(2,1)} %bitcast.43, bf16[512,1024]{1,0:T(8,128)(2,1)} %bitcast.46, ...), custom_call_target="tpu_custom_call" | custom-call | tf_op jit(solution)/shard_map/expert/pallas_call | solution.py:248
  83.2 0.0 copy-start.4
  83.2 3.7 %all-to-all-start.2 = ((bf16[4,1536,128]{2,1,0:T(8,128)(2,1)}), bf16[4,1536,128]{2,1,0:T(8,128)(2,1)S(1)}, u32[]{:S(2)}, u32[]{:S(2)}) async-start(bf16[4,1536,128]{2,1,0:T(8,128)(2,1)} %get-tuple-element.16), calls=%async_computation.2 | async-start | bytes 3145728 | tf_op jit(solution)/shard_map/all_to_all | solution.py:298
  86.9 0.0 copy-done.4
  86.9 2.7 %convolution_convert_fusion = bf16[512,1024]{1,0:T(8,128)(2,1)} fusion(bf16[384,1024]{1,0:T(8,128)(2,1)S(1)} %copy-done.4, bf16[2,384,512]{2,1,0:T(8,128)(2,1)} %get-tuple-element.26), kind=kOutput, calls=%fused_computation.2 | convolution fusion | flops 403177472 | bytes 2228224 | tf_op jit(solution)/shard_map/dot_general | solution.py:21
  89.6 1.9 %collective-permute-start.3 = (bf16[512,1024]{1,0:T(8,128)(2,1)}, bf16[512,1024]{1,0:T(8,128)(2,1)S(1)}, u32[]{:S(2)}, u32[]{:S(2)}) collective-permute-start(bf16[512,1024]{1,0:T(8,128)(2,1)} %convolution_convert_fusion), channel_id=1, source_target_pairs={{0,64},{64,0},{1,65},{65,1},{2,66},{66,2},{3,67},{67,3},{4,68},{68... | collective-permute-start | bytes 3145736 | tf_op jit(solution)/shard_map/ppermute | solution.py:304
  91.5 16.4 %all-to-all-done.2.parts_ref = bf16[4,1536,128]{2,1,0:T(8,128)(2,1)S(1)} async-done(((bf16[4,1536,128]{2,1,0:T(8,128)(2,1)}), bf16[4,1536,128]{2,1,0:T(8,128)(2,1)S(1)}, u32[]{:S(2)}, u32[]{:S(2)}) %all-to-all-start.2) | async-done | bytes 1572896 | tf_op jit(solution)/shard_map/all_to_all | solution.py:298
  107.9 0.2 fold.1
  108.1 0.9 copy.13
  109.0 0.0 copy-start.5
  109.0 0.0 copy-start.6
  109.0 8.3 %all-to-all-start.3 = ((bf16[128,3,4,128]{3,2,1,0:T(4,128)(2,1)}), bf16[128,3,4,128]{3,2,1,0:T(4,128)(2,1)S(1)}, u32[]{:S(2)}, u32[]{:S(2)}) async-start(bf16[128,3,4,128]{3,2,1,0:T(4,128)(2,1)} %bitcast.33), calls=%async_computation.3 | async-start | bytes 786432 | tf_op jit(solution)/shard_map/all_to_all | solution.py:302
  117.3 2.0 %convolution_convert_fusion.1 = bf16[1024,512]{1,0:T(8,128)(2,1)S(1)} fusion(bf16[384,1024]{1,0:T(8,128)(2,1)} %get-tuple-element.24, bf16[2,384,512]{2,1,0:T(8,128)(2,1)} %get-tuple-element.25), kind=kOutput, calls=%fused_computation.3 | convolution fusion | flops 403177472 | bytes 2228224 | tf_op jit(solution)/shard_map/dot_general | solution.py:21
  119.2 0.0 copy-start.7
  119.3 0.0 copy-start.8
  119.3 2.6 %collective-permute-start.2 = (bf16[1024,512]{1,0:T(8,128)(2,1)S(1)}, bf16[1024,512]{1,0:T(8,128)(2,1)S(1)}, u32[]{:S(2)}, u32[]{:S(2)}) collective-permute-start(bf16[1024,512]{1,0:T(8,128)(2,1)S(1)} %convolution_convert_fusion.1), channel_id=1, source_target_pairs={{0,64},{64,0},{1,65},{65,1},{2,66},{66,2},{3,67},{67,3},{4,68},{68... | collective-permute-start | bytes 3145736 | tf_op jit(solution)/shard_map/ppermute | solution.py:305
  121.9 0.0 collective-permute-done.3
  121.9 0.0 copy-done.5
  121.9 0.0 copy-done.6
  121.9 1.7 %fusion.1 = bf16[1,512,1024]{2,1,0:T(8,128)(2,1)} fusion(bf16[512,1024]{1,0:T(8,128)(2,1)S(1)} %collective-permute-done.3, bf16[384,1024]{1,0:T(8,128)(2,1)S(1)} %copy-done.5, bf16[2,384,512]{2,1,0:T(8,128)(2,1)S(1)} %copy-done.6), kind=kOutput, calls=%fused_computation.5 | convolution fusion | flops 404226048 | bytes 3276800 | tf_op jit(solution)/shard_map/dot_general | solution.py:21
  123.6 0.0 copy-start
  123.6 0.0 copy-start.1
  123.6 0.5 collective-permute-done.2
  124.1 0.0 copy-done.7
  124.1 0.0 copy-done.8
  124.1 1.7 %fusion = bf16[1,1024,512]{2,1,0:T(8,128)(2,1)} fusion(bf16[1024,512]{1,0:T(8,128)(2,1)S(1)} %collective-permute-done.2, bf16[384,1024]{1,0:T(8,128)(2,1)S(1)} %copy-done.7, bf16[2,384,512]{2,1,0:T(8,128)(2,1)S(1)} %copy-done.8), kind=kOutput, calls=%fused_computation.4 | convolution fusion | flops 404226048 | bytes 3276800 | tf_op jit(solution)/shard_map/dot_general | solution.py:21
  125.9 0.0 copy-done
  125.9 0.0 copy-done.1
  125.9 1.1 route.1
  127.0 15.1 %all-to-all-done.3 = bf16[128,3,4,128]{3,2,1,0:T(4,128)(2,1)S(1)} async-done(((bf16[128,3,4,128]{3,2,1,0:T(4,128)(2,1)}), bf16[128,3,4,128]{3,2,1,0:T(4,128)(2,1)S(1)}, u32[]{:S(2)}, u32[]{:S(2)}) %all-to-all-start.3) | async-done | bytes 393248 | tf_op jit(solution)/shard_map/all_to_all | solution.py:302
  142.0 1.3 combine.1
Async XLA Ops:
  48.8 4.6 %copy-start.2 = (bf16[1,1024,512]{2,1,0:T(8,128)(2,1)S(1)}, bf16[1,1024,512]{2,1,0:T(8,128)(2,1)}, u32[]{:S(2)}) copy-start(bf16[1,1024,512]{2,1,0:T(8,128)(2,1)} %param.10) | copy-start | bytes 3145732
  48.8 26.5 %all-to-all-start.1 = ((bf16[4,1536,128]{2,1,0:T(8,128)(2,1)}), bf16[4,1536,128]{2,1,0:T(8,128)(2,1)S(1)}, u32[]{:S(2)}, u32[]{:S(2)}) async-start(bf16[4,1536,128]{2,1,0:T(8,128)(2,1)} %broadcast_in_dim.14), calls=%async_computation.1 | async-start | bytes 3145728 | tf_op jit(solution)/shard_map/all_to_all | solution.py:296
  53.4 4.9 %collective-permute-start = (bf16[1024,512]{1,0:T(8,128)(2,1)S(1)}, bf16[1024,512]{1,0:T(8,128)(2,1)S(1)}, u32[]{:S(2)}, u32[]{:S(2)}) collective-permute-start(bf16[1024,512]{1,0:T(8,128)(2,1)S(1)} %bitcast.44), channel_id=1, source_target_pairs={{0,64},{64,0},{1,65},{65,1},{2,66},{66,2},{3,67},{67,3},{4,68},{68... | collective-permute-start | bytes 3145736 | tf_op jit(solution)/shard_map/weights/ppermute | solution.py:292
  56.0 4.9 %collective-permute-start.1 = (bf16[512,1024]{1,0:T(8,128)(2,1)}, bf16[512,1024]{1,0:T(8,128)(2,1)}, u32[]{:S(2)}, u32[]{:S(2)}) collective-permute-start(bf16[512,1024]{1,0:T(8,128)(2,1)} %bitcast.45), channel_id=1, source_target_pairs={{0,64},{64,0},{1,65},{65,1},{2,66},{66,2},{3,67},{67,3},{4,68},{68... | collective-permute-start | bytes 3145736 | tf_op jit(solution)/shard_map/weights/ppermute | solution.py:293
  58.3 1.0 copy-start.3
  83.2 3.7 %copy-start.4 = (bf16[384,1024]{1,0:T(8,128)(2,1)S(1)}, bf16[384,1024]{1,0:T(8,128)(2,1)}, u32[]{:S(2)}) copy-start(bf16[384,1024]{1,0:T(8,128)(2,1)} %get-tuple-element.27) | copy-start | bytes 2359300
  83.2 24.7 %all-to-all-start.2 = ((bf16[4,1536,128]{2,1,0:T(8,128)(2,1)}), bf16[4,1536,128]{2,1,0:T(8,128)(2,1)S(1)}, u32[]{:S(2)}, u32[]{:S(2)}) async-start(bf16[4,1536,128]{2,1,0:T(8,128)(2,1)} %get-tuple-element.16), calls=%async_computation.2 | async-start | bytes 3145728 | tf_op jit(solution)/shard_map/all_to_all | solution.py:298
  89.6 32.3 %collective-permute-start.3 = (bf16[512,1024]{1,0:T(8,128)(2,1)}, bf16[512,1024]{1,0:T(8,128)(2,1)S(1)}, u32[]{:S(2)}, u32[]{:S(2)}) collective-permute-start(bf16[512,1024]{1,0:T(8,128)(2,1)} %convolution_convert_fusion), channel_id=1, source_target_pairs={{0,64},{64,0},{1,65},{65,1},{2,66},{66,2},{3,67},{67,3},{4,68},{68... | collective-permute-start | bytes 3145736 | tf_op jit(solution)/shard_map/ppermute | solution.py:304
  109.0 12.9 %copy-start.5 = (bf16[384,1024]{1,0:T(8,128)(2,1)S(1)}, bf16[384,1024]{1,0:T(8,128)(2,1)}, u32[]{:S(2)}) copy-start(bf16[384,1024]{1,0:T(8,128)(2,1)} %get-tuple-element.27) | copy-start | bytes 2359300
  109.0 12.9 %copy-start.6 = (bf16[2,384,512]{2,1,0:T(8,128)(2,1)S(1)}, bf16[2,384,512]{2,1,0:T(8,128)(2,1)}, u32[]{:S(2)}) copy-start(bf16[2,384,512]{2,1,0:T(8,128)(2,1)} %get-tuple-element.26) | copy-start | bytes 2359300
  109.0 33.1 %all-to-all-start.3 = ((bf16[128,3,4,128]{3,2,1,0:T(4,128)(2,1)}), bf16[128,3,4,128]{3,2,1,0:T(4,128)(2,1)S(1)}, u32[]{:S(2)}, u32[]{:S(2)}) async-start(bf16[128,3,4,128]{3,2,1,0:T(4,128)(2,1)} %bitcast.33), calls=%async_computation.3 | async-start | bytes 786432 | tf_op jit(solution)/shard_map/all_to_all | solution.py:302
  119.2 4.9 %copy-start.7 = (bf16[384,1024]{1,0:T(8,128)(2,1)S(1)}, bf16[384,1024]{1,0:T(8,128)(2,1)}, u32[]{:S(2)}) copy-start(bf16[384,1024]{1,0:T(8,128)(2,1)} %get-tuple-element.24) | copy-start | bytes 2359300
  119.3 4.9 %copy-start.8 = (bf16[2,384,512]{2,1,0:T(8,128)(2,1)S(1)}, bf16[2,384,512]{2,1,0:T(8,128)(2,1)}, u32[]{:S(2)}) copy-start(bf16[2,384,512]{2,1,0:T(8,128)(2,1)} %get-tuple-element.25) | copy-start | bytes 2359300
  119.3 4.9 %collective-permute-start.2 = (bf16[1024,512]{1,0:T(8,128)(2,1)S(1)}, bf16[1024,512]{1,0:T(8,128)(2,1)S(1)}, u32[]{:S(2)}, u32[]{:S(2)}) collective-permute-start(bf16[1024,512]{1,0:T(8,128)(2,1)S(1)} %convolution_convert_fusion.1), channel_id=1, source_target_pairs={{0,64},{64,0},{1,65},{65,1},{2,66},{66,2},{3,67},{67,3},{4,68},{68... | collective-permute-start | bytes 3145736 | tf_op jit(solution)/shard_map/ppermute | solution.py:305
  123.6 2.3 %copy-start = (s32[256,2]{0,1:T(2,128)S(1)}, s32[256,2]{0,1:T(2,128)}, u32[]{:S(2)}) copy-start(s32[256,2]{0,1:T(2,128)} %param.8) | copy-start | bytes 6148
  123.6 2.3 %copy-start.1 = (f32[256,2]{0,1:T(2,128)S(1)}, f32[256,2]{0,1:T(2,128)}, u32[]{:S(2)}) copy-start(f32[256,2]{0,1:T(2,128)} %param.9) | copy-start | bytes 6148

commit v4 on v3

--- a/solution.py
+++ b/solution.py
@@ -291,13 +291,16 @@
     with jax.named_scope("weights"):
         other_in = lax.ppermute(w_in, "core", swap)
         other_out = lax.ppermute(w_out, "core", swap)
+    got, other_in, other_out = lax.optimization_barrier((got, other_in, other_out))
     got = jnp.transpose(got, (1, 0, 2, 3)).reshape(1, -1, width)
     got = jnp.broadcast_to(got, (n_y,) + got.shape[1:])
     got = lax.all_to_all(got, "y", 0, 0, tiled=True)
     part, x, s, h, d = expert_work(got, w_in, w_out, other_in, other_out)
     summed = fold(lax.all_to_all(part, "y", 0, 0, tiled=True))
     summed = jnp.transpose(summed.reshape(chunks[1], chunks[0], 4, width), (1, 0, 2, 3))
-    summed, ids, gates = lax.optimization_barrier((summed, expert_ids, gate_weights))
+    summed, ids, gates, x, s, h, d = lax.optimization_barrier(
+        (summed, expert_ids, gate_weights, x, s, h, d)
+    )
     pick, gate = route(ids, gates, experts, width)
     ret = lax.all_to_all(summed, CXZ, 0, 0, tiled=True).reshape(-1, width)
     output, grad_tokens = combine(pick, gate, ret, rows)

time: 146 us -> 143 us (0.979)
  waiting for transfers between devices: 48.3 us -> 34.4 us
  starting transfers between devices: 25.6 us -> 36.7 us
  blocking collectives: 44.1 us -> 49.6 us
  matrix products: 8.1 us -> 4.9 us
  local copies, waits for them, and re-layouts: 3.4 us -> 1.28 us
    all_to_all x2 -> x1, waiting for transfers between devices: 30.7 us -> 17.5 us  [on_device(): got = lax.all_to_all(send.reshape(chunks), CXZ, 0, 0, tiled=True)]
    all_to_all x2 -> x1, starting transfers between devices: 8.3 us -> 19.6 us  [on_device(): got = lax.all_to_all(send.reshape(chunks), CXZ, 0, 0, tiled=True)]
    all_to_all x1 -> x2, blocking collectives: 44.1 us -> 49.6 us  [the longest x1 26.1 us: on_device(): got = lax.all_to_all(got, 'y', 0, 0, tiled=True)]
    dot_general x4, matrix products: 8.1 us -> 4.9 us  [dot(): lax.dot_general(left, right, (((left_dim,), (right_dim,)), ((), ())), pre...]
  transfers between devices with their start and end apart: 7 -> 6, of which waited for: 6 -> 4; matrix products, arithmetic and copies ran while one was open for 6% -> 3% of each run, Pallas kernels for 1% -> 1%
where the time goes in v4:
time: 143 us; the launch traced here: 140 us
  blocking collectives  49.6 us (35%)
  starting transfers between devices  36.7 us (26%)
  waiting for transfers between devices  34.4 us (24%)
  Pallas kernels  12.5 us (9%)
  matrix products  4.9 us (3%)
    all_to_all x1, blocking collectives, on_device(): got = lax.all_to_all(got, 'y', 0, 0, tiled=True)  26.1 us
    all_to_all x1, blocking collectives, on_device(): summed = fold(lax.all_to_all(part, 'y', 0, 0, tiled=True))  23.5 us
    all_to_all x1, starting transfers between devices, on_device(): got = lax.all_to_all(send.reshape(chunks), CXZ, 0, 0, tiled=True)  19.6 us
    all_to_all x1, waiting for transfers between devices, on_device(): got = lax.all_to_all(send.reshape(chunks), CXZ, 0, 0, tiled=True)  17.5 us
    all_to_all x1, waiting for transfers between devices, on_device(): ret = lax.all_to_all(summed, CXZ, 0, 0, tiled=True).reshape(-1, width)  14.1 us
    all_to_all x1, starting transfers between devices, on_device(): ret = lax.all_to_all(summed, CXZ, 0, 0, tiled=True).reshape(-1, width)  8.25 us
    pallas_call x1, Pallas kernels, expert_work(): pl.pallas_call(expert_kernel, in_specs=[vmem] + [hbm] * 4, out_specs=[vme...  6.64 us
    dot_general x4, matrix products, dot(): lax.dot_general(left, right, (((left_dim,), (right_dim,)), ((), ())), pre...  4.9 us
  transfers between devices with their start and end apart: 6, of which 4 were waited for; matrix products, arithmetic and copies ran while one was open for 3% of the time, Pallas kernels for 1%

profile of v4, /device:TPU:6, one launch (start us, length us, event | category | flops | bytes accessed | tf_op | source)
XLA Modules:
  0.0 140.3 jit_solution(2159658002024021898)
XLA Ops:
  0.6 3.3 %dispatch.1 = bf16[1536,128]{1,0:T(8,128)(2,1)} custom-call(s32[2,256]{1,0:T(2,128)} %bitcast.40, f32[2,256]{1,0:T(2,128)} %bitcast.42, bf16[256,128]{1,0:T(8,128)(2,1)} %tok_hbm.1, bf16[256,128]{1,0:T(8,128)(2,1)} %cot_hbm.1), custom_call_target="tpu_custom_call" | custom-call | tf_op jit(solution)/shard_map/dispatch/pallas_call | solution.py:100
  3.9 19.6 %all-to-all-start = ((bf16[128,3,4,128]{3,2,1,0:T(4,128)(2,1)}), bf16[128,3,4,128]{3,2,1,0:T(4,128)(2,1)S(1)}, u32[]{:S(2)}, u32[]{:S(2)}) async-start(bf16[128,3,4,128]{3,2,1,0:T(4,128)(2,1)} %bitcast.2), calls=%async_computation | async-start | bytes 786432 | tf_op jit(solution)/shard_map/to_experts/all_to_all | solution.py:290
  23.5 2.5 %collective-permute-start = (bf16[1024,512]{1,0:T(8,128)(2,1)}, bf16[1024,512]{1,0:T(8,128)(2,1)S(1)}, u32[]{:S(2)}, u32[]{:S(2)}) collective-permute-start(bf16[1024,512]{1,0:T(8,128)(2,1)} %bitcast.46), channel_id=1, source_target_pairs={{0,64},{64,0},{1,65},{65,1},{2,66},{66,2},{3,67},{67,3},{4,68},{68... | collective-permute-start | bytes 3145736 | tf_op jit(solution)/shard_map/weights/ppermute | solution.py:292
  26.0 1.9 %collective-permute-start.1 = (bf16[512,1024]{1,0:T(8,128)(2,1)}, bf16[512,1024]{1,0:T(8,128)(2,1)S(1)}, u32[]{:S(2)}, u32[]{:S(2)}) collective-permute-start(bf16[512,1024]{1,0:T(8,128)(2,1)} %bitcast.48), channel_id=1, source_target_pairs={{0,64},{64,0},{1,65},{65,1},{2,66},{66,2},{3,67},{67,3},{4,68},{68... | collective-permute-start | bytes 3145736 | tf_op jit(solution)/shard_map/weights/ppermute | solution.py:293
  27.9 0.5 collective-permute-done.win1
  28.4 0.0 copy-start.2
  28.4 2.3 %collective-permute-done.1.wout1 = bf16[512,1024]{1,0:T(8,128)(2,1)S(1)} collective-permute-done((bf16[512,1024]{1,0:T(8,128)(2,1)}, bf16[512,1024]{1,0:T(8,128)(2,1)S(1)}, u32[]{:S(2)}, u32[]{:S(2)}) %collective-permute-start.1) | collective-permute-done | bytes 1048608 | tf_op jit(solution)/shard_map/weights/ppermute | solution.py:293
  30.7 0.0 copy-start.3
  30.7 17.5 %all-to-all-done = bf16[128,3,4,128]{3,2,1,0:T(4,128)(2,1)S(1)} async-done(((bf16[128,3,4,128]{3,2,1,0:T(4,128)(2,1)}), bf16[128,3,4,128]{3,2,1,0:T(4,128)(2,1)S(1)}, u32[]{:S(2)}, u32[]{:S(2)}) %all-to-all-start) | async-done | bytes 393248 | tf_op jit(solution)/shard_map/to_experts/all_to_all | solution.py:290
  48.2 0.1 copy.10
  48.4 0.2 broadcast_in_dim.14
  48.6 26.1 %all_to_all.20.got_ref = bf16[4,1536,128]{2,1,0:T(8,128)(2,1)S(1)} all-to-all(bf16[4,1536,128]{2,1,0:T(8,128)(2,1)S(1)} %broadcast_in_dim.14), channel_id=1, replica_groups=mesh['y'=4,'core'=2,'x'=4,'z'=16] {'y'}, dimensions={0} | all-to-all | bytes 3145728 | tf_op jit(solution)/shard_map/all_to_all | solution.py:297
  74.7 0.0 copy-done.2
  74.7 0.0 copy-done.3
  74.7 6.6 %expert.1 = (bf16[4,1536,128]{2,1,0:T(8,128)(2,1)S(1)}, bf16[384,1024]{1,0:T(8,128)(2,1)}, bf16[384,1024]{1,0:T(8,128)(2,1)}, bf16[2,384,512]{2,1,0:T(8,128)(2,1)}, bf16[2,384,512]{2,1,0:T(8,128)(2,1)}) custom-call(bf16[4,1536,128]{2,1,0:T(8,128)(2,1)S(1)} %all_to_all.20.got_ref, bf16[1024,512]{1,0:T(8,128)(2,1)} %bitcast.47, bf16[512,1024]{1,0:T(8,128)(2,1)} %bitcast.49, ...), custom_call_target="tpu_custom_call" | custom-call | tf_op jit(solution)/shard_map/expert/pallas_call | solution.py:248
  81.4 23.5 %all_to_all.21.parts_ref = bf16[4,1536,128]{2,1,0:T(8,128)(2,1)S(1)} all-to-all(bf16[4,1536,128]{2,1,0:T(8,128)(2,1)S(1)} %get-tuple-element.26), channel_id=1, replica_groups=mesh['y'=4,'core'=2,'x'=4,'z'=16] {'y'}, dimensions={0} | all-to-all | bytes 3145728 | tf_op jit(solution)/shard_map/all_to_all | solution.py:299
  104.9 0.0 copy-start.4
  104.9 0.0 copy-start.5
  104.9 0.2 fold.1
  105.1 0.9 copy.13
  106.0 0.0 copy-start.7
  106.0 0.0 copy-start.9
  106.0 8.3 %all-to-all-start.3 = ((bf16[128,3,4,128]{3,2,1,0:T(4,128)(2,1)}), bf16[128,3,4,128]{3,2,1,0:T(4,128)(2,1)S(1)}, u32[]{:S(2)}, u32[]{:S(2)}) async-start(bf16[128,3,4,128]{3,2,1,0:T(4,128)(2,1)} %bitcast.37), calls=%async_computation.3 | async-start | bytes 786432 | tf_op jit(solution)/shard_map/all_to_all | solution.py:305
  114.2 0.0 copy-done.4
  114.2 0.0 copy-done.5
  114.2 0.7 convolution_convert_fusion
  115.0 0.0 copy-start
  115.0 0.0 copy-start.1
  115.0 0.0 copy-start.6
  115.0 2.6 %collective-permute-start.3 = (bf16[512,1024]{1,0:T(8,128)(2,1)S(1)}, bf16[512,1024]{1,0:T(8,128)(2,1)S(1)}, u32[]{:S(2)}, u32[]{:S(2)}) collective-permute-start(bf16[512,1024]{1,0:T(8,128)(2,1)S(1)} %convolution_convert_fusion), channel_id=1, source_target_pairs={{0,64},{64,0},{1,65},{65,1},{2,66},{66,2},{3,67},{67,3},{4,68},{68... | collective-permute-start | bytes 3145736 | tf_op jit(solution)/shard_map/ppermute | solution.py:307
  117.6 0.0 copy-done.7
  117.6 0.0 copy-done.9
  117.6 0.7 convolution_convert_fusion.1
  118.4 1.9 %collective-permute-start.2 = (bf16[1024,512]{1,0:T(8,128)(2,1)S(1)}, bf16[1024,512]{1,0:T(8,128)(2,1)S(1)}, u32[]{:S(2)}, u32[]{:S(2)}) collective-permute-start(bf16[1024,512]{1,0:T(8,128)(2,1)S(1)} %convolution_convert_fusion.1), channel_id=1, source_target_pairs={{0,64},{64,0},{1,65},{65,1},{2,66},{66,2},{3,67},{67,3},{4,68},{68... | collective-permute-start | bytes 3145736 | tf_op jit(solution)/shard_map/ppermute | solution.py:308
  120.3 0.0 copy-done
  120.3 0.0 copy-done.1
  120.3 1.1 route.1
  121.4 0.0 copy-start.8
  121.4 0.0 copy-start.10
  121.4 0.0 collective-permute-done.3
  121.4 0.0 copy-done.6
  121.5 1.7 %fusion.1 = bf16[1,512,1024]{2,1,0:T(8,128)(2,1)} fusion(bf16[512,1024]{1,0:T(8,128)(2,1)S(1)} %collective-permute-done.3, bf16[384,1024]{1,0:T(8,128)(2,1)S(1)} %copy-done.4, bf16[2,384,512]{2,1,0:T(8,128)(2,1)S(1)} %copy-done.6), kind=kOutput, calls=%fused_computation.5 | convolution fusion | flops 404226048 | bytes 3276800 | tf_op jit(solution)/shard_map/dot_general | solution.py:21
  123.2 0.0 collective-permute-done.2
  123.2 0.0 copy-done.8
  123.2 0.0 copy-done.10
  123.2 1.7 %fusion = bf16[1,1024,512]{2,1,0:T(8,128)(2,1)} fusion(bf16[1024,512]{1,0:T(8,128)(2,1)S(1)} %collective-permute-done.2, bf16[384,1024]{1,0:T(8,128)(2,1)S(1)} %copy-done.8, bf16[2,384,512]{2,1,0:T(8,128)(2,1)S(1)} %copy-done.10), kind=kOutput, calls=%fused_computation.4 | convolution fusion | flops 404226048 | bytes 3276800 | tf_op jit(solution)/shard_map/dot_general | solution.py:21
  124.9 14.1 %all-to-all-done.3 = bf16[128,3,4,128]{3,2,1,0:T(4,128)(2,1)S(1)} async-done(((bf16[128,3,4,128]{3,2,1,0:T(4,128)(2,1)}), bf16[128,3,4,128]{3,2,1,0:T(4,128)(2,1)S(1)}, u32[]{:S(2)}, u32[]{:S(2)}) %all-to-all-start.3) | async-done | bytes 393248 | tf_op jit(solution)/shard_map/all_to_all | solution.py:305
  139.0 1.3 combine.1
Async XLA Ops:
  3.9 44.3 %all-to-all-start = ((bf16[128,3,4,128]{3,2,1,0:T(4,128)(2,1)}), bf16[128,3,4,128]{3,2,1,0:T(4,128)(2,1)S(1)}, u32[]{:S(2)}, u32[]{:S(2)}) async-start(bf16[128,3,4,128]{3,2,1,0:T(4,128)(2,1)} %bitcast.2), calls=%async_computation | async-start | bytes 786432 | tf_op jit(solution)/shard_map/to_experts/all_to_all | solution.py:290
  23.5 4.9 %collective-permute-start = (bf16[1024,512]{1,0:T(8,128)(2,1)}, bf16[1024,512]{1,0:T(8,128)(2,1)S(1)}, u32[]{:S(2)}, u32[]{:S(2)}) collective-permute-start(bf16[1024,512]{1,0:T(8,128)(2,1)} %bitcast.46), channel_id=1, source_target_pairs={{0,64},{64,0},{1,65},{65,1},{2,66},{66,2},{3,67},{67,3},{4,68},{68... | collective-permute-start | bytes 3145736 | tf_op jit(solution)/shard_map/weights/ppermute | solution.py:292
  26.0 4.8 %collective-permute-start.1 = (bf16[512,1024]{1,0:T(8,128)(2,1)}, bf16[512,1024]{1,0:T(8,128)(2,1)S(1)}, u32[]{:S(2)}, u32[]{:S(2)}) collective-permute-start(bf16[512,1024]{1,0:T(8,128)(2,1)} %bitcast.48), channel_id=1, source_target_pairs={{0,64},{64,0},{1,65},{65,1},{2,66},{66,2},{3,67},{67,3},{4,68},{68... | collective-permute-start | bytes 3145736 | tf_op jit(solution)/shard_map/weights/ppermute | solution.py:293
  28.4 46.3 %copy-start.2 = (bf16[1024,512]{1,0:T(8,128)(2,1)}, bf16[1024,512]{1,0:T(8,128)(2,1)S(1)}, u32[]{:S(2)}) copy-start(bf16[1024,512]{1,0:T(8,128)(2,1)S(1)} %collective-permute-done.win1) | copy-start | bytes 3145732
  30.7 44.0 %copy-start.3 = (bf16[512,1024]{1,0:T(8,128)(2,1)}, bf16[512,1024]{1,0:T(8,128)(2,1)S(1)}, u32[]{:S(2)}) copy-start(bf16[512,1024]{1,0:T(8,128)(2,1)S(1)} %collective-permute-done.1.wout1) | copy-start | bytes 3145732
  104.9 9.4 %copy-start.4 = (bf16[384,1024]{1,0:T(8,128)(2,1)S(1)}, bf16[384,1024]{1,0:T(8,128)(2,1)}, u32[]{:S(2)}) copy-start(bf16[384,1024]{1,0:T(8,128)(2,1)} %get-tuple-element.41) | copy-start | bytes 2359300
  104.9 9.4 %copy-start.5 = (bf16[2,384,512]{2,1,0:T(8,128)(2,1)S(1)}, bf16[2,384,512]{2,1,0:T(8,128)(2,1)}, u32[]{:S(2)}) copy-start(bf16[2,384,512]{2,1,0:T(8,128)(2,1)} %get-tuple-element.40) | copy-start | bytes 2359300
  106.0 11.7 %copy-start.7 = (bf16[384,1024]{1,0:T(8,128)(2,1)S(1)}, bf16[384,1024]{1,0:T(8,128)(2,1)}, u32[]{:S(2)}) copy-start(bf16[384,1024]{1,0:T(8,128)(2,1)} %get-tuple-element.38) | copy-start | bytes 2359300
  106.0 11.7 %copy-start.9 = (bf16[2,384,512]{2,1,0:T(8,128)(2,1)S(1)}, bf16[2,384,512]{2,1,0:T(8,128)(2,1)}, u32[]{:S(2)}) copy-start(bf16[2,384,512]{2,1,0:T(8,128)(2,1)} %get-tuple-element.39) | copy-start | bytes 2359300
  106.0 33.0 %all-to-all-start.3 = ((bf16[128,3,4,128]{3,2,1,0:T(4,128)(2,1)}), bf16[128,3,4,128]{3,2,1,0:T(4,128)(2,1)S(1)}, u32[]{:S(2)}, u32[]{:S(2)}) async-start(bf16[128,3,4,128]{3,2,1,0:T(4,128)(2,1)} %bitcast.37), calls=%async_computation.3 | async-start | bytes 786432 | tf_op jit(solution)/shard_map/all_to_all | solution.py:305
  115.0 5.3 %copy-start = (s32[256,2]{0,1:T(2,128)S(1)}, s32[256,2]{0,1:T(2,128)}, u32[]{:S(2)}) copy-start(s32[256,2]{0,1:T(2,128)} %param.8) | copy-start | bytes 6148
  115.0 5.3 %copy-start.1 = (f32[256,2]{0,1:T(2,128)S(1)}, f32[256,2]{0,1:T(2,128)}, u32[]{:S(2)}) copy-start(f32[256,2]{0,1:T(2,128)} %param.9) | copy-start | bytes 6148
  115.0 6.5 %copy-start.6 = (bf16[2,384,512]{2,1,0:T(8,128)(2,1)S(1)}, bf16[2,384,512]{2,1,0:T(8,128)(2,1)}, u32[]{:S(2)}) copy-start(bf16[2,384,512]{2,1,0:T(8,128)(2,1)} %get-tuple-element.40) | copy-start | bytes 2359300
  115.0 6.4 %collective-permute-start.3 = (bf16[512,1024]{1,0:T(8,128)(2,1)S(1)}, bf16[512,1024]{1,0:T(8,128)(2,1)S(1)}, u32[]{:S(2)}, u32[]{:S(2)}) collective-permute-start(bf16[512,1024]{1,0:T(8,128)(2,1)S(1)} %convolution_convert_fusion), channel_id=1, source_target_pairs={{0,64},{64,0},{1,65},{65,1},{2,66},{66,2},{3,67},{67,3},{4,68},{68... | collective-permute-start | bytes 3145736 | tf_op jit(solution)/shard_map/ppermute | solution.py:307
  118.4 4.8 %collective-permute-start.2 = (bf16[1024,512]{1,0:T(8,128)(2,1)S(1)}, bf16[1024,512]{1,0:T(8,128)(2,1)S(1)}, u32[]{:S(2)}, u32[]{:S(2)}) collective-permute-start(bf16[1024,512]{1,0:T(8,128)(2,1)S(1)} %convolution_convert_fusion.1), channel_id=1, source_target_pairs={{0,64},{64,0},{1,65},{65,1},{2,66},{66,2},{3,67},{67,3},{4,68},{68... | collective-permute-start | bytes 3145736 | tf_op jit(solution)/shard_map/ppermute | solution.py:308
  121.4 1.8 %copy-start.8 = (bf16[384,1024]{1,0:T(8,128)(2,1)S(1)}, bf16[384,1024]{1,0:T(8,128)(2,1)}, u32[]{:S(2)}) copy-start(bf16[384,1024]{1,0:T(8,128)(2,1)} %get-tuple-element.38) | copy-start | bytes 2359300
  121.4 1.7 %copy-start.10 = (bf16[2,384,512]{2,1,0:T(8,128)(2,1)S(1)}, bf16[2,384,512]{2,1,0:T(8,128)(2,1)}, u32[]{:S(2)}) copy-start(bf16[2,384,512]{2,1,0:T(8,128)(2,1)} %get-tuple-element.39) | copy-start | bytes 2359300

commit v5 on v4

--- a/solution.py
+++ b/solution.py
@@ -55,7 +55,8 @@
     return chunk - experts * core, slot, is_input
 
 
-def dispatch_kernel(ids_hbm, gates_hbm, tok_hbm, cot_hbm, send_ref, ids_ref, gates_ref, tok_ref, cot_ref, sems):
+def dispatch_kernel(ids_hbm, gates_hbm, tok_hbm, cot_hbm, send_hbm, ids_ref, gates_ref, tok_ref, cot_ref, send_ref, sems, out_sems):
+    writes, parts = [], out_sems.shape[0]
     copies = fetch(
         ((ids_hbm, ids_ref), (gates_hbm, gates_ref), (tok_hbm, tok_ref), (cot_hbm, cot_ref)), sems
     )
@@ -74,7 +75,6 @@
     ranks = jnp.concatenate(
         [jnp.where(first, rank, -1.0), jnp.where(second, rank, -1.0)], axis=1
     ).astype(bf16)
-    pick = ones_where(dot(owner, ranks) == slot.astype(f32))
     for copy in copies[1:]:
         copy.wait()
     gates = columns(gates_ref[...])
@@ -87,8 +87,17 @@
         ],
         axis=0,
     )
-    both = dot(pick, source)
-    send_ref[...] = jnp.where(is_input, both[:, :width], both[:, width:]).astype(bf16)
+    slot = slot.astype(f32)
+    step = n_send // parts
+    for i in range(parts):
+        at = slice(i * step, (i + 1) * step)
+        both = dot(ones_where(dot(owner[at], ranks) == slot[at]), source)
+        send_ref[at] = jnp.where(is_input[at], both[:, :width], both[:, width:]).astype(bf16)
+        write = pltpu.make_async_copy(send_ref.at[at], send_hbm.at[at], out_sems.at[i])
+        write.start()
+        writes.append(write)
+    for write in writes:
+        write.wait()
 
 
 def in_hbm(*arrays):
@@ -100,12 +109,15 @@
     return pl.pallas_call(
         dispatch_kernel,
         in_specs=[pl.BlockSpec(memory_space=pltpu.HBM)] * 4,
-        out_shape=jax.ShapeDtypeStruct((2 * experts * CHUNK, width), bf16),
+        out_specs=pl.BlockSpec(memory_space=pltpu.HBM),
+        out_shape=pltpu.HBM((2 * experts * CHUNK, width), bf16),
         scratch_shapes=[
             pltpu.VMEM((2, rows), jnp.int32),
             pltpu.VMEM((2, rows), f32),
             pltpu.VMEM((rows, width), bf16),
             pltpu.VMEM((rows, width), bf16),
+            pltpu.VMEM((2 * experts * CHUNK, width), bf16),
+            pltpu.SemaphoreType.DMA((4,)),
             pltpu.SemaphoreType.DMA((4,)),
         ],
         compiler_params=pltpu.CompilerParams(vmem_limit_bytes=16 << 20),
@@ -174,14 +186,10 @@
 
 
 def expert_kernel(got_ref, win0, wout0, win1, wout1, part_ref, x_hbm, s_hbm, h_hbm, d_hbm, win_ref, wout_ref, x_ref, s_ref, h_ref, d_ref, sems):
-    weights = fetch(
-        (
-            (win0, win_ref.at[0]),
-            (win1, win_ref.at[1]),
-            (wout0, wout_ref.at[0]),
-            (wout1, wout_ref.at[1]),
-        ),
-        sems,
+    weights = fetch(((win0, win_ref.at[0]), (wout0, wout_ref.at[0])), sems)
+    later = (
+        pltpu.make_async_copy(win1, win_ref.at[1], sems.at[2]),
+        pltpu.make_async_copy(wout1, wout_ref.at[1], sems.at[3]),
     )
     n_y, n_rows, width = got_ref.shape
     group = n_rows // 3
@@ -207,13 +215,16 @@
         save.start()
     out = back = None
     for c in range(2):
-        weights[c].wait()
+        (weights[0] if c == 0 else later[0]).wait()
+        if c == 0:
+            for copy in later:
+                copy.start()
         pre = dot(x_ref[...], win_ref[c])
         cdf = 0.5 * (1.0 + lax.erf(pre * half_root))
         hidden = (pre * cdf).astype(bf16)
         h_ref[c] = hidden
         slope = cdf + pre * inv_root_tau * jnp.exp(-0.5 * pre * pre)
-        weights[2 + c].wait()
+        (weights[1] if c == 0 else later[1]).wait()
         d_pre = (dot(s_ref[...], wout_ref[c], 1, 1) * slope).astype(bf16)
         d_ref[c] = d_pre
         for save in (
@@ -264,15 +275,31 @@
     )(got, *in_hbm(w_in, w_out, other_in, other_out))
 
 
-def fold_kernel(parts_ref, out_ref):
-    parts = [parts_ref[y].astype(f32) for y in range(parts_ref.shape[0])]
-    out_ref[...] = sum(parts[1:], parts[0]).astype(bf16)
+def fold_kernel(parts_ref, out_hbm, sum_ref, sems):
+    n_y, n_rows, width = parts_ref.shape
+    step = n_rows // 3
+    writes = []
+    for k in range(3):
+        at = slice(k * step, (k + 1) * step)
+        parts = [parts_ref[y, at].astype(f32) for y in range(n_y)]
+        sum_ref[k] = sum(parts[1:], parts[0]).reshape(step // 4, 4, width).astype(bf16)
+        write = pltpu.make_async_copy(sum_ref.at[k], out_hbm.at[:, k], sems.at[k])
+        write.start()
+        writes.append(write)
+    for write in writes:
+        write.wait()
 
 
 def fold(parts):
+    _, n_rows, width = parts.shape
     return pl.pallas_call(
         fold_kernel,
-        out_shape=jax.ShapeDtypeStruct(parts.shape[1:], bf16),
+        out_specs=pl.BlockSpec(memory_space=pltpu.HBM),
+        out_shape=pltpu.HBM((n_rows // CHUNK, 3, 4, width), bf16),
+        scratch_shapes=[
+            pltpu.VMEM((3, n_rows // CHUNK, 4, width), bf16),
+            pltpu.SemaphoreType.DMA((3,)),
+        ],
         compiler_params=pltpu.CompilerParams(vmem_limit_bytes=12 << 20),
         name="fold",
     )(parts)
@@ -297,7 +324,6 @@
     got = lax.all_to_all(got, "y", 0, 0, tiled=True)
     part, x, s, h, d = expert_work(got, w_in, w_out, other_in, other_out)
     summed = fold(lax.all_to_all(part, "y", 0, 0, tiled=True))
-    summed = jnp.transpose(summed.reshape(chunks[1], chunks[0], 4, width), (1, 0, 2, 3))
     summed, ids, gates, x, s, h, d = lax.optimization_barrier(
         (summed, expert_ids, gate_weights, x, s, h, d)
     )

time: 143 us -> 142 us (level)
  transfers between devices with their start and end apart: 6 -> 6, of which waited for: 4 -> 4; matrix products, arithmetic and copies ran while one was open for 3% -> 4% of each run, Pallas kernels for 1% -> 1%
where the time goes in v5:
time: 142 us; the launch traced here: 140 us
  blocking collectives  49.6 us (35%)
  starting transfers between devices  36.9 us (26%)
  waiting for transfers between devices  34.2 us (24%)
  Pallas kernels  12.7 us (9%)
  matrix products  4.9 us (3%)
    all_to_all x1, blocking collectives, on_device(): got = lax.all_to_all(got, 'y', 0, 0, tiled=True)  26.1 us
    all_to_all x1, blocking collectives, on_device(): summed = fold(lax.all_to_all(part, 'y', 0, 0, tiled=True))  23.5 us
    all_to_all x1, starting transfers between devices, on_device(): got = lax.all_to_all(send.reshape(chunks), CXZ, 0, 0, tiled=True)  19.6 us
    all_to_all x1, waiting for transfers between devices, on_device(): got = lax.all_to_all(send.reshape(chunks), CXZ, 0, 0, tiled=True)  17.5 us
    all_to_all x1, waiting for transfers between devices, on_device(): ret = lax.all_to_all(summed, CXZ, 0, 0, tiled=True).reshape(-1, width)  13.9 us
    all_to_all x1, starting transfers between devices, on_device(): ret = lax.all_to_all(summed, CXZ, 0, 0, tiled=True).reshape(-1, width)  8.26 us
    pallas_call x1, Pallas kernels, expert_work(): pl.pallas_call(expert_kernel, in_specs=[vmem] + [hbm] * 4, out_specs=[vme...  6.32 us
    dot_general x4, matrix products, dot(): lax.dot_general(left, right, (((left_dim,), (right_dim,)), ((), ())), pre...  4.9 us
  transfers between devices with their start and end apart: 6, of which 4 were waited for; matrix products, arithmetic and copies ran while one was open for 4% of the time, Pallas kernels for 1%

profile of v5, /device:TPU:6, one launch (start us, length us, event | category | flops | bytes accessed | tf_op | source)
XLA Modules:
  0.0 139.6 jit_solution(18329069433863840360)
XLA Ops:
  0.6 3.0 %dispatch.1 = bf16[1536,128]{1,0:T(8,128)(2,1)} custom-call(s32[2,256]{1,0:T(2,128)} %bitcast.35, f32[2,256]{1,0:T(2,128)} %bitcast.37, bf16[256,128]{1,0:T(8,128)(2,1)} %tok_hbm.1, bf16[256,128]{1,0:T(8,128)(2,1)} %cot_hbm.1), custom_call_target="tpu_custom_call" | custom-call | tf_op jit(solution)/shard_map/dispatch/pallas_call | solution.py:109
  3.6 19.6 %all-to-all-start = ((bf16[128,3,4,128]{3,2,1,0:T(4,128)(2,1)}), bf16[128,3,4,128]{3,2,1,0:T(4,128)(2,1)S(1)}, u32[]{:S(2)}, u32[]{:S(2)}) async-start(bf16[128,3,4,128]{3,2,1,0:T(4,128)(2,1)} %bitcast.40), calls=%async_computation | async-start | bytes 786432 | tf_op jit(solution)/shard_map/to_experts/all_to_all | solution.py:317
  23.2 2.5 %collective-permute-start = (bf16[1024,512]{1,0:T(8,128)(2,1)}, bf16[1024,512]{1,0:T(8,128)(2,1)S(1)}, u32[]{:S(2)}, u32[]{:S(2)}) collective-permute-start(bf16[1024,512]{1,0:T(8,128)(2,1)} %bitcast.42), channel_id=1, source_target_pairs={{0,64},{64,0},{1,65},{65,1},{2,66},{66,2},{3,67},{67,3},{4,68},{68... | collective-permute-start | bytes 3145736 | tf_op jit(solution)/shard_map/weights/ppermute | solution.py:319
  25.7 1.9 %collective-permute-start.1 = (bf16[512,1024]{1,0:T(8,128)(2,1)}, bf16[512,1024]{1,0:T(8,128)(2,1)S(1)}, u32[]{:S(2)}, u32[]{:S(2)}) collective-permute-start(bf16[512,1024]{1,0:T(8,128)(2,1)} %bitcast.44), channel_id=1, source_target_pairs={{0,64},{64,0},{1,65},{65,1},{2,66},{66,2},{3,67},{67,3},{4,68},{68... | collective-permute-start | bytes 3145736 | tf_op jit(solution)/shard_map/weights/ppermute | solution.py:320
  27.6 0.5 collective-permute-done.win1
  28.2 0.0 copy-start.2
  28.2 2.3 %collective-permute-done.1.wout1 = bf16[512,1024]{1,0:T(8,128)(2,1)S(1)} collective-permute-done((bf16[512,1024]{1,0:T(8,128)(2,1)}, bf16[512,1024]{1,0:T(8,128)(2,1)S(1)}, u32[]{:S(2)}, u32[]{:S(2)}) %collective-permute-start.1) | collective-permute-done | bytes 1048608 | tf_op jit(solution)/shard_map/weights/ppermute | solution.py:320
  30.5 0.0 copy-start.3
  30.5 17.5 %all-to-all-done = bf16[128,3,4,128]{3,2,1,0:T(4,128)(2,1)S(1)} async-done(((bf16[128,3,4,128]{3,2,1,0:T(4,128)(2,1)}), bf16[128,3,4,128]{3,2,1,0:T(4,128)(2,1)S(1)}, u32[]{:S(2)}, u32[]{:S(2)}) %all-to-all-start) | async-done | bytes 393248 | tf_op jit(solution)/shard_map/to_experts/all_to_all | solution.py:317
  48.0 0.1 copy.10
  48.1 0.2 broadcast_in_dim.14
  48.3 26.1 %all_to_all.20.got_ref = bf16[4,1536,128]{2,1,0:T(8,128)(2,1)S(1)} all-to-all(bf16[4,1536,128]{2,1,0:T(8,128)(2,1)S(1)} %broadcast_in_dim.14), channel_id=1, replica_groups=mesh['y'=4,'core'=2,'x'=4,'z'=16] {'y'}, dimensions={0} | all-to-all | bytes 3145728 | tf_op jit(solution)/shard_map/all_to_all | solution.py:324
  74.5 0.0 copy-done.2
  74.5 0.0 copy-done.3
  74.5 6.3 %expert.1 = (bf16[4,1536,128]{2,1,0:T(8,128)(2,1)S(1)}, bf16[384,1024]{1,0:T(8,128)(2,1)}, bf16[384,1024]{1,0:T(8,128)(2,1)}, bf16[2,384,512]{2,1,0:T(8,128)(2,1)}, bf16[2,384,512]{2,1,0:T(8,128)(2,1)}) custom-call(bf16[4,1536,128]{2,1,0:T(8,128)(2,1)S(1)} %all_to_all.20.got_ref, bf16[1024,512]{1,0:T(8,128)(2,1)} %bitcast.43, bf16[512,1024]{1,0:T(8,128)(2,1)} %bitcast.45, ...), custom_call_target="tpu_custom_call" | custom-call | tf_op jit(solution)/shard_map/expert/pallas_call | solution.py:259
  80.8 23.5 %all_to_all.21.parts_ref = bf16[4,1536,128]{2,1,0:T(8,128)(2,1)S(1)} all-to-all(bf16[4,1536,128]{2,1,0:T(8,128)(2,1)S(1)} %get-tuple-element.26), channel_id=1, replica_groups=mesh['y'=4,'core'=2,'x'=4,'z'=16] {'y'}, dimensions={0} | all-to-all | bytes 3145728 | tf_op jit(solution)/shard_map/all_to_all | solution.py:326
  104.3 0.0 copy-start.4
  104.3 0.0 copy-start.5
  104.3 1.0 fold.1
  105.2 0.0 copy-start.7
  105.2 0.0 copy-start.9
  105.2 8.3 %all-to-all-start.3 = ((bf16[128,3,4,128]{3,2,1,0:T(4,128)(2,1)}), bf16[128,3,4,128]{3,2,1,0:T(4,128)(2,1)S(1)}, u32[]{:S(2)}, u32[]{:S(2)}) async-start(bf16[128,3,4,128]{3,2,1,0:T(4,128)(2,1)} %fold.1), calls=%async_computation.3 | async-start | bytes 786432 | tf_op jit(solution)/shard_map/all_to_all | solution.py:331
  113.5 0.0 copy-done.4
  113.5 0.0 copy-done.5
  113.5 0.7 convolution_convert_fusion
  114.3 0.0 copy-start
  114.3 0.0 copy-start.1
  114.3 0.0 copy-start.6
  114.3 2.8 %collective-permute-start.3 = (bf16[512,1024]{1,0:T(8,128)(2,1)S(1)}, bf16[512,1024]{1,0:T(8,128)(2,1)S(1)}, u32[]{:S(2)}, u32[]{:S(2)}) collective-permute-start(bf16[512,1024]{1,0:T(8,128)(2,1)S(1)} %convolution_convert_fusion), channel_id=1, source_target_pairs={{0,64},{64,0},{1,65},{65,1},{2,66},{66,2},{3,67},{67,3},{4,68},{68... | collective-permute-start | bytes 3145736 | tf_op jit(solution)/shard_map/ppermute | solution.py:333
  117.1 0.0 copy-done.7
  117.1 0.0 copy-done.9
  117.1 0.7 convolution_convert_fusion.1
  117.9 1.9 %collective-permute-start.2 = (bf16[1024,512]{1,0:T(8,128)(2,1)S(1)}, bf16[1024,512]{1,0:T(8,128)(2,1)S(1)}, u32[]{:S(2)}, u32[]{:S(2)}) collective-permute-start(bf16[1024,512]{1,0:T(8,128)(2,1)S(1)} %convolution_convert_fusion.1), channel_id=1, source_target_pairs={{0,64},{64,0},{1,65},{65,1},{2,66},{66,2},{3,67},{67,3},{4,68},{68... | collective-permute-start | bytes 3145736 | tf_op jit(solution)/shard_map/ppermute | solution.py:334
  119.8 0.0 copy-done
  119.8 0.0 copy-done.1
  119.8 1.1 route.1
  120.9 0.0 copy-start.8
  120.9 0.0 copy-start.10
  120.9 0.0 collective-permute-done.3
  120.9 0.0 copy-done.6
  120.9 1.7 %fusion.1 = bf16[1,512,1024]{2,1,0:T(8,128)(2,1)} fusion(bf16[512,1024]{1,0:T(8,128)(2,1)S(1)} %collective-permute-done.3, bf16[384,1024]{1,0:T(8,128)(2,1)S(1)} %copy-done.4, bf16[2,384,512]{2,1,0:T(8,128)(2,1)S(1)} %copy-done.6), kind=kOutput, calls=%fused_computation.5 | convolution fusion | flops 404226048 | bytes 3276800 | tf_op jit(solution)/shard_map/dot_general | solution.py:21
  122.7 0.0 collective-permute-done.2
  122.7 0.0 copy-done.8
  122.7 0.0 copy-done.10
  122.7 1.7 %fusion = bf16[1,1024,512]{2,1,0:T(8,128)(2,1)} fusion(bf16[1024,512]{1,0:T(8,128)(2,1)S(1)} %collective-permute-done.2, bf16[384,1024]{1,0:T(8,128)(2,1)S(1)} %copy-done.8, bf16[2,384,512]{2,1,0:T(8,128)(2,1)S(1)} %copy-done.10), kind=kOutput, calls=%fused_computation.4 | convolution fusion | flops 404226048 | bytes 3276800 | tf_op jit(solution)/shard_map/dot_general | solution.py:21
  124.4 13.9 %all-to-all-done.3 = bf16[128,3,4,128]{3,2,1,0:T(4,128)(2,1)S(1)} async-done(((bf16[128,3,4,128]{3,2,1,0:T(4,128)(2,1)}), bf16[128,3,4,128]{3,2,1,0:T(4,128)(2,1)S(1)}, u32[]{:S(2)}, u32[]{:S(2)}) %all-to-all-start.3) | async-done | bytes 393248 | tf_op jit(solution)/shard_map/all_to_all | solution.py:331
  138.3 1.3 combine.1
Async XLA Ops:
  3.6 44.3 %all-to-all-start = ((bf16[128,3,4,128]{3,2,1,0:T(4,128)(2,1)}), bf16[128,3,4,128]{3,2,1,0:T(4,128)(2,1)S(1)}, u32[]{:S(2)}, u32[]{:S(2)}) async-start(bf16[128,3,4,128]{3,2,1,0:T(4,128)(2,1)} %bitcast.40), calls=%async_computation | async-start | bytes 786432 | tf_op jit(solution)/shard_map/to_experts/all_to_all | solution.py:317
  23.2 4.9 %collective-permute-start = (bf16[1024,512]{1,0:T(8,128)(2,1)}, bf16[1024,512]{1,0:T(8,128)(2,1)S(1)}, u32[]{:S(2)}, u32[]{:S(2)}) collective-permute-start(bf16[1024,512]{1,0:T(8,128)(2,1)} %bitcast.42), channel_id=1, source_target_pairs={{0,64},{64,0},{1,65},{65,1},{2,66},{66,2},{3,67},{67,3},{4,68},{68... | collective-permute-start | bytes 3145736 | tf_op jit(solution)/shard_map/weights/ppermute | solution.py:319
  25.7 4.8 %collective-permute-start.1 = (bf16[512,1024]{1,0:T(8,128)(2,1)}, bf16[512,1024]{1,0:T(8,128)(2,1)S(1)}, u32[]{:S(2)}, u32[]{:S(2)}) collective-permute-start(bf16[512,1024]{1,0:T(8,128)(2,1)} %bitcast.44), channel_id=1, source_target_pairs={{0,64},{64,0},{1,65},{65,1},{2,66},{66,2},{3,67},{67,3},{4,68},{68... | collective-permute-start | bytes 3145736 | tf_op jit(solution)/shard_map/weights/ppermute | solution.py:320
  28.2 46.3 %copy-start.2 = (bf16[1024,512]{1,0:T(8,128)(2,1)}, bf16[1024,512]{1,0:T(8,128)(2,1)S(1)}, u32[]{:S(2)}) copy-start(bf16[1024,512]{1,0:T(8,128)(2,1)S(1)} %collective-permute-done.win1) | copy-start | bytes 3145732
  30.5 44.0 %copy-start.3 = (bf16[512,1024]{1,0:T(8,128)(2,1)}, bf16[512,1024]{1,0:T(8,128)(2,1)S(1)}, u32[]{:S(2)}) copy-start(bf16[512,1024]{1,0:T(8,128)(2,1)S(1)} %collective-permute-done.1.wout1) | copy-start | bytes 3145732
  104.3 9.3 %copy-start.4 = (bf16[384,1024]{1,0:T(8,128)(2,1)S(1)}, bf16[384,1024]{1,0:T(8,128)(2,1)}, u32[]{:S(2)}) copy-start(bf16[384,1024]{1,0:T(8,128)(2,1)} %get-tuple-element.41) | copy-start | bytes 2359300
  104.3 9.3 %copy-start.5 = (bf16[2,384,512]{2,1,0:T(8,128)(2,1)S(1)}, bf16[2,384,512]{2,1,0:T(8,128)(2,1)}, u32[]{:S(2)}) copy-start(bf16[2,384,512]{2,1,0:T(8,128)(2,1)} %get-tuple-element.40) | copy-start | bytes 2359300
  105.2 11.9 %copy-start.7 = (bf16[384,1024]{1,0:T(8,128)(2,1)S(1)}, bf16[384,1024]{1,0:T(8,128)(2,1)}, u32[]{:S(2)}) copy-start(bf16[384,1024]{1,0:T(8,128)(2,1)} %get-tuple-element.38) | copy-start | bytes 2359300
  105.2 11.9 %copy-start.9 = (bf16[2,384,512]{2,1,0:T(8,128)(2,1)S(1)}, bf16[2,384,512]{2,1,0:T(8,128)(2,1)}, u32[]{:S(2)}) copy-start(bf16[2,384,512]{2,1,0:T(8,128)(2,1)} %get-tuple-element.39) | copy-start | bytes 2359300
  105.2 33.0 %all-to-all-start.3 = ((bf16[128,3,4,128]{3,2,1,0:T(4,128)(2,1)}), bf16[128,3,4,128]{3,2,1,0:T(4,128)(2,1)S(1)}, u32[]{:S(2)}, u32[]{:S(2)}) async-start(bf16[128,3,4,128]{3,2,1,0:T(4,128)(2,1)} %fold.1), calls=%async_computation.3 | async-start | bytes 786432 | tf_op jit(solution)/shard_map/all_to_all | solution.py:331
  114.3 5.5 %copy-start = (s32[256,2]{0,1:T(2,128)S(1)}, s32[256,2]{0,1:T(2,128)}, u32[]{:S(2)}) copy-start(s32[256,2]{0,1:T(2,128)} %param.8) | copy-start | bytes 6148
  114.3 5.5 %copy-start.1 = (f32[256,2]{0,1:T(2,128)S(1)}, f32[256,2]{0,1:T(2,128)}, u32[]{:S(2)}) copy-start(f32[256,2]{0,1:T(2,128)} %param.9) | copy-start | bytes 6148
  114.3 6.6 %copy-start.6 = (bf16[2,384,512]{2,1,0:T(8,128)(2,1)S(1)}, bf16[2,384,512]{2,1,0:T(8,128)(2,1)}, u32[]{:S(2)}) copy-start(bf16[2,384,512]{2,1,0:T(8,128)(2,1)} %get-tuple-element.40) | copy-start | bytes 2359300
  114.3 6.6 %collective-permute-start.3 = (bf16[512,1024]{1,0:T(8,128)(2,1)S(1)}, bf16[512,1024]{1,0:T(8,128)(2,1)S(1)}, u32[]{:S(2)}, u32[]{:S(2)}) collective-permute-start(bf16[512,1024]{1,0:T(8,128)(2,1)S(1)} %convolution_convert_fusion), channel_id=1, source_target_pairs={{0,64},{64,0},{1,65},{65,1},{2,66},{66,2},{3,67},{67,3},{4,68},{68... | collective-permute-start | bytes 3145736 | tf_op jit(solution)/shard_map/ppermute | solution.py:333
  117.9 4.8 %collective-permute-start.2 = (bf16[1024,512]{1,0:T(8,128)(2,1)S(1)}, bf16[1024,512]{1,0:T(8,128)(2,1)S(1)}, u32[]{:S(2)}, u32[]{:S(2)}) collective-permute-start(bf16[1024,512]{1,0:T(8,128)(2,1)S(1)} %convolution_convert_fusion.1), channel_id=1, source_target_pairs={{0,64},{64,0},{1,65},{65,1},{2,66},{66,2},{3,67},{67,3},{4,68},{68... | collective-permute-start | bytes 3145736 | tf_op jit(solution)/shard_map/ppermute | solution.py:334
  120.9 1.8 %copy-start.8 = (bf16[384,1024]{1,0:T(8,128)(2,1)S(1)}, bf16[384,1024]{1,0:T(8,128)(2,1)}, u32[]{:S(2)}) copy-start(bf16[384,1024]{1,0:T(8,128)(2,1)} %get-tuple-element.38) | copy-start | bytes 2359300
  120.9 1.8 %copy-start.10 = (bf16[2,384,512]{2,1,0:T(8,128)(2,1)S(1)}, bf16[2,384,512]{2,1,0:T(8,128)(2,1)}, u32[]{:S(2)}) copy-start(bf16[2,384,512]{2,1,0:T(8,128)(2,1)} %get-tuple-element.39) | copy-start | bytes 2359300
